TPU v7x, 32 devices: a whole 2x2x4 slice. The times are simulated.
32 devices in a mesh: groups: 2 (over x), chan: 16 (over z, y, core).
Axes of the slice: x: 2, y: 2, z: 4, core: 2. Of those that a mesh axis runs over, the one named last changes fastest.
Arguments:
- samples: bfloat16 [512, 2048], P(('groups', 'chan')), parts along dimension 0, may hold values from -6 to 6
- scales: bfloat16 [512], P(('groups', 'chan')), parts along dimension 0, may hold values from 0.5 to 2
- bin_ids: int32 [16, 16], replicated, may hold values from 0 to 15, as said below
- owner_table: int32 [16], replicated, may hold values from 0 to 15, each once
Outputs:
- stacks: float32 [32, 16640], P(('groups', 'chan')), parts along dimension 0
There are 2 independent parts, one for each index of `groups`. A program takes and returns all parts, laid end to end along the dimension named above; an argument that names none is the same for every part. Nothing has to cross between parts.
Inputs may be any that keep to these rules, and one draw needn't show every extreme that they name: `bin_ids`: each bin holds at most 32 tiles, and some bin exactly 32; every bin holds at least one. `owner_table`: each device owns exactly one bin.
All inputs are finite; a program needn't handle non-finite values.
Results may differ from a plain program's by a relative error of at most 0.0003.
Values may be sent and summed in bfloat16 or wider, within the bound.
No kernel may reach another device: no remote copies, remote signals or barrier semaphores. Data moves between devices by JAX's collectives and lax.ppermute only.
A program may use at most 64 MiB of HBM per device.

v0:
```python
import jax
import jax.numpy as jnp
from jax import lax
from jax.sharding import PartitionSpec as P

LAG = 32
LAGS = 65


def unfold(record):
    span_len = record.shape[1] - 2 * LAG
    middle = record[:, LAG : LAG + span_len]
    stacked = jnp.stack(
        [jnp.pad(middle, ((0, 0), (offset, 2 * LAG - offset))) for offset in range(LAGS)], axis=1
    )
    return stacked.reshape(record.shape[0] * LAGS, record.shape[1])


def lookup_many(values, positions):
    hits = jnp.arange(values.shape[0], dtype=jnp.int32)[None, :] == positions[:, None]
    return jnp.sum(jnp.where(hits, values[None, :], 0), axis=1)


def on_device(samples, scales, bin_ids, owner_table):
    per_dev = samples.shape[0]
    span_len = samples.shape[1] - 2 * LAG
    devices = lax.axis_size("chan")
    own_index = lax.axis_index("chan")
    own_bin = jnp.sum(
        jnp.where(owner_table == own_index, jnp.arange(owner_table.shape[0], dtype=jnp.int32), 0)
    )
    bin_count = jnp.sum((bin_ids == own_bin).astype(jnp.float32))
    unfolded = unfold(samples)
    own_scales = scales.astype(jnp.float32)
    row_bins = lax.dynamic_index_in_dim(bin_ids, own_index, 0, keepdims=False)
    row_slots = lookup_many(owner_table, row_bins)
    initial = jnp.zeros((devices, per_dev, LAGS, per_dev), jnp.float32)
    record = lax.all_gather(samples, "chan", axis=0, tiled=True)
    record_scales = lax.all_gather(scales, "chan", axis=0, tiled=True)
    rows_now = record.shape[0]
    products = lax.dot_general(
        unfolded, record, (((1,), (1,)), ((), ())), preferred_element_type=jnp.float32
    )
    shaped = products.reshape(per_dev, LAGS, record.shape[0])
    tile_now = shaped * own_scales[:, None, None] * record_scales.astype(jnp.float32)[None, None, :]
    channel = jnp.arange(rows_now, dtype=jnp.int32)
    slot_ids = lookup_many(row_slots, channel // per_dev)
    running = initial.at[slot_ids, :, :, channel % per_dev].add(tile_now.transpose(2, 0, 1))
    summed = lax.psum_scatter(running, "chan", scatter_dimension=0, tiled=True)
    stacks = summed / jnp.sqrt(bin_count * span_len)
    return stacks.reshape(1, per_dev * LAGS * per_dev)


def solution(mesh):
    placed = (P(("groups", "chan"), None), P(("groups", "chan")), P(), P())
    return jax.shard_map(
        on_device,
        mesh=mesh,
        in_specs=placed,
        out_specs=P(("groups", "chan"), None),
        check_vma=False,
    )
```

profile of v0, /device:TPU:0, one launch (start us, length us, event | category | flops | bytes accessed | tf_op | source)
XLA Modules:
  0.0 204.4 jit_solution(13227517512175597422)
XLA Ops:
  6.5 0.7 all-gather.2.cloned.1.call-update
  7.3 0.9 slice.3
  8.2 0.4 pad_bitcast_fusion.38
  8.8 0.1 copy.2126
  8.9 0.1 copy.2127
  9.1 0.1 copy.2129
  10.8 0.4 pad_bitcast_fusion.19
  12.1 0.7 copy.2152
  12.8 0.8 copy.2153
  13.6 0.7 copy.2154
  14.3 0.8 copy.2155
  15.1 0.7 copy.2156
  15.8 0.7 copy.2157
  16.6 0.7 copy.2158
  17.3 0.7 copy.2159
  18.0 0.7 copy.2160
  18.8 0.7 copy.2161
  19.5 0.7 copy.2162
  20.3 0.4 pad_bitcast_fusion
  20.7 0.8 copy.2163
  21.5 0.8 copy.2164
  22.2 0.7 copy.2165
  23.0 0.7 copy.2166
  23.7 0.7 copy.2167
  24.4 0.8 copy.2168
  25.2 0.8 copy.2169
  25.9 0.8 copy.2170
  26.7 0.8 copy.2171
  27.5 0.8 copy.2172
  28.2 0.7 copy.2173
  29.0 0.7 copy.2174
  29.7 0.8 copy.2175
  30.5 0.7 copy.2176
  31.2 0.8 copy.2177
  32.0 0.8 copy.2178
  32.7 0.8 copy.2179
  33.5 0.7 copy.2180
  34.2 0.8 copy.2181
  35.0 0.2 pad_bitcast_fusion.57
  35.2 0.8 copy.2117
  35.9 0.8 copy.2118
  36.7 0.8 copy.2119
  37.4 0.8 copy.2120
  38.2 0.7 copy.2121
  38.9 0.8 copy.2122
  39.7 0.8 copy.2123
  40.4 0.8 copy.2124
  41.2 0.5 convert_element_type.139
  41.7 0.6 dynamic-slice
  43.0 0.2 dynamic-update-slice
  43.2 35.1 %all-reduce.65 = bf16[256]{0:T(256)(128)(2,1)S(1)} all-reduce(bf16[256]{0:T(256)(128)(2,1)S(1)} %dynamic-update-slice), channel_id=1, replica_groups=mesh['groups'=2,'chan'=16] {'chan'}, use_global_device_ids=true, to_apply=%add.65 | all-reduce | flops 256 | bytes 1024
  78.4 29.3 %stack.263 = bf16[16,65,2048]{2,1,0:T(8,128)(2,1)} concatenate(bf16[16,1,2048]{2,1,0:T(2,128)(2,1)} %copy.2117, bf16[16,1,2048]{2,1,0:T(2,128)(2,1)} %copy.2118, bf16[16,1,2048]{2,1,0:T(2,128)(2,1)} %copy.2119, bf16[16,1,2048]{2,1,0:T(2,128)(2,1)} %copy.2120, bf16[16,1,2048]{2,1,0:T(2,128)(2,1)} %copy.2121, bf16[16,1,2048]{2,1,0:T(2,128)(2,1)} %copy.2122, ...), dimensions={1} | concatenate | bytes 8519680 | tf_op jit(solution)/shard_map/stack | solution.py:13
  107.7 0.2 select_reduce_fusion.1
  108.1 4.1 %fusion.1 = f32[256,16,65]{0,2,1:T(8,128)S(1)} fusion(bf16[16,65,2048]{2,1,0:T(8,128)(2,1)} %stack.263, bf16[256,2048]{1,0:T(8,128)(2,1)} %all-gather.2.cloned.1.call-done, f32[256]{0:T(256)S(1)} %convert_element_type.140, f32[16]{0:T(128)} %convert_element_type.139), kind=kOutput, calls=%fused_computation.3 | convolution fusion | flops 1091051520 | bytes 6374464 | tf_op jit(solution)/shard_map/dot_general | solution.py:41
  112.2 2.0 copy.2182
  114.2 0.2 broadcast_in_dim.41
  114.4 20.5 %scatter_fusion = f32[16,16,65,16]{2,1,3,0:T(8,128)S(1)} fusion(f32[16,16,65,16]{2,1,3,0:T(8,128)S(1)} %broadcast_in_dim.41, s32[256]{0:T(256)S(1)} %bitcast.141, f32[256,16,65]{2,1,0:T(8,128)} %copy.2182), kind=kCustom, calls=%fused_computation | custom fusion | flops 266240 | bytes 3196928 | tf_op jit(solution)/shard_map/scatter-add | solution.py:48
  134.9 1.3 copy-done
  136.3 0.6 fusion.4
  137.0 1.3 convert_reduce_fusion
  139.0 56.5 %reduce-scatter.2.cloned.1.call-done = f32[1,16,65,16]{2,1,3,0:T(8,128)} async-done(((f32[16,16,65,16]{2,1,3,0:T(8,128)}), f32[1,16,65,16]{2,1,3,0:T(8,128)}) %reduce-scatter.2.cloned.1.call-update) | async-done | bytes 66576 | tf_op jit(solution)/shard_map/reduce_scatter | solution.py:49
  195.5 0.9 broadcast_divide_fusion
  196.4 0.3 copy.2183
  196.7 0.9 reshape.70
  (43 shorter events, 2.7 us)
Async XLA Ops:
  6.5 101.5 %all-gather.2.cloned.1.call-start = ((), (), s32[]{:S(2)}) async-start(), calls=%async_computation.1 | async-start | bytes 1114112 | tf_op jit(solution)/shard_map/all_gather | solution.py:38
  7.3 188.3 %reduce-scatter.2.cloned.1.call-start = ((), (), s32[]{:S(2)}) async-start(), calls=%async_computation.2 | async-start | bytes 2228224 | tf_op jit(solution)/shard_map/reduce_scatter | solution.py:49
  27.5 13.7 %copy-start.2 = (bf16[16]{0:T(256)(128)(2,1)S(1)}, bf16[16]{0:T(256)(128)(2,1)}, u32[]{:S(2)}) copy-start(bf16[16]{0:T(256)(128)(2,1)} %param.5) | copy-start | bytes 100
  27.5 14.3 %copy-start.4 = (u32[32]{0:T(128)S(1)}, u32[32]{0:T(128)}, u32[]{:S(2)}) copy-start(u32[32]{0:T(128)} %constant.199) | copy-start | bytes 388
  78.4 29.3 %copy-start.1 = (s32[16,16]{1,0:T(8,128)S(1)}, s32[16,16]{1,0:T(8,128)}, u32[]{:S(2)}) copy-start(s32[16,16]{1,0:T(8,128)} %param.6) | copy-start | bytes 3076
  78.4 29.4 %copy-start.3 = (s32[16]{0:T(128)S(1)}, s32[16]{0:T(128)}, u32[]{:S(2)}) copy-start(s32[16]{0:T(128)} %param.7) | copy-start | bytes 196
  134.9 1.4 copy-start
Sparse Core Ops, SparseCore 0:
  9.5 40.5 all-gather.1
  136.4 59.0 reduce-scatter.1
where the time goes:
time: 206 us; the launch traced here: 204 us
  local copies, waits for them, and re-layouts  68.5 us (33%)
  waiting for transfers between devices  57.3 us (28%)
  blocking collectives  35.1 us (17%)
  other arithmetic  24.2 us (12%)
  between operations  15.1 us (7%)
  matrix products  4.11 us (2%)
    another operation x70, local copies, waits for them, and re-layouts, unfold(): jnp.stack([jnp.pad(middle, ((0, 0), (offset, 2 * LAG - offset))) for offs...  62 us
    reduce_scatter x1, waiting for transfers between devices, on_device(): summed = lax.psum_scatter(running, 'chan', scatter_dimension=0, tiled=True)  56.5 us
    unnamed x1, blocking collectives  35.1 us
    scatter-add x1, other arithmetic, on_device(): initial.at[slot_ids, :, :, channel % per_dev]  20.5 us
  transfers between devices with their start and end apart: 2, of which 1 were waited for; matrix products, arithmetic and copies ran while one was open for 33% of the time, Pallas kernels for 0%

commit v1 on v0

v1 whole, which is shorter than its diff:
```python
import functools

import jax
import jax.numpy as jnp
from jax import lax
from jax.experimental import pallas as pl
from jax.experimental.pallas import tpu as pltpu
from jax.sharding import PartitionSpec as P

LAG = 32
LAGS = 65
CH = 16
STEP = 16
LANES = CH * STEP
FINE = 8
COARSE = 16
ROWS = FINE * COARSE
HEAD = ROWS + 8
REACH = LAG // STEP
SHIFTS = 2 * REACH + 1
OUT_LANES = LAGS * CH

VMEM = pl.BlockSpec(memory_space=pltpu.VMEM)
SMEM = pl.BlockSpec(memory_space=pltpu.SMEM)
ANY = pl.BlockSpec(memory_space=pl.ANY)


def piece_offset(devices, index):
    far = devices // 4
    return (
        lax.rem(index, far) * 4 + lax.rem(lax.div(index, far), 2) * 2 + lax.div(index, 2 * far)
    )


def prep_kernel(samples_ref, scales_ref, piece_ref, turned_ref):
    samples = samples_ref[...].astype(jnp.float32)
    for u2 in range(COARSE):
        turned_ref[u2 * 128 : (u2 + 1) * 128, 0:CH] = samples[:, u2 * 128 : (u2 + 1) * 128].T
    for u1 in range(FINE):
        parts = [
            turned_ref[pl.ds(STEP * u1 + v, COARSE, stride=128), 0:CH] for v in range(STEP)
        ]
        piece_ref[u1 * COARSE : (u1 + 1) * COARSE, :] = jnp.concatenate(parts, axis=1).astype(
            jnp.bfloat16
        )
    scales = scales_ref[...].astype(jnp.float32)
    piece_ref[ROWS:HEAD, :] = jnp.broadcast_to(
        jnp.concatenate([scales] * STEP, axis=1), (HEAD - ROWS, LANES)
    ).astype(jnp.bfloat16)


def prep(samples, scales):
    return pl.pallas_call(
        prep_kernel,
        out_shape=jax.ShapeDtypeStruct((HEAD, LANES), jnp.bfloat16),
        in_specs=[VMEM, VMEM],
        out_specs=VMEM,
        scratch_shapes=[pltpu.VMEM((COARSE * 128, 128), jnp.float32)],
        compiler_params=pltpu.CompilerParams(vmem_limit_bytes=8 << 20),
        name="prep",
    )(samples, scales.reshape(1, CH))


def pairs_kernel(devices, own_ref, bins_ref, owner_ref, list_ref):
    own = own_ref[0]
    own_bin = jnp.int32(0)
    for i in range(devices):
        own_bin = jnp.where(owner_ref[i] == own, i, own_bin)

    def row(i, found):
        list_ref[i] = found
        p = own ^ piece_offset(devices, i)
        for j in range(devices):
            q = own ^ piece_offset(devices, jnp.int32(j))
            list_ref[devices + 1 + found] = j
            found = found + jnp.where(bins_ref[p, q] == own_bin, 1, 0)
        return found

    list_ref[devices] = lax.fori_loop(0, devices, row, jnp.int32(0))


def find_pairs(devices, own, bin_ids, owner_table):
    return pl.pallas_call(
        functools.partial(pairs_kernel, devices),
        out_shape=jax.ShapeDtypeStruct((devices + 1 + devices * devices + 1,), jnp.int32),
        in_specs=[SMEM] * 3,
        out_specs=SMEM,
        compiler_params=pltpu.CompilerParams(vmem_limit_bytes=1 << 20),
        name="pairs",
    )(own, bin_ids, owner_table)


def split(value):
    high = value.astype(jnp.bfloat16)
    return high, (value - high.astype(jnp.float32)).astype(jnp.bfloat16)


def stack_kernel(
    devices, span, list_ref, near_ref, far_ref, out_ref, x_ref, ah_ref, al_ref, at_ref, yh_ref, yl_ref, sem
):
    half = devices // 2
    depth = devices * ROWS
    slab = devices * COARSE
    copies = [
        pltpu.make_async_copy(near_ref, x_ref.at[pl.ds(0, half)], sem.at[0]),
        pltpu.make_async_copy(far_ref, x_ref.at[pl.ds(half, half)], sem.at[1]),
    ]
    for copy in copies:
        copy.start()
    row = lax.broadcasted_iota(jnp.int32, (ROWS, LANES), 0)
    fine, coarse = row // COARSE, row % COARSE
    u = FINE * coarse + fine
    inside = (u >= REACH) & (u < ROWS - REACH)
    for i in range(devices):
        if i % half == 0:
            copies[i // half].wait()
        scale = x_ref[i, ROWS : ROWS + 1, :].astype(jnp.float32)
        value = jnp.where(inside, x_ref[i, 0:ROWS, :].astype(jnp.float32) * scale, 0.0)
        high, low = split(value)
        for u1 in range(FINE):
            at = (u1 * devices + i) * COARSE
            ah_ref[at : at + COARSE, :] = high[u1 * COARSE : (u1 + 1) * COARSE]
            al_ref[at : at + COARSE, :] = low[u1 * COARSE : (u1 + 1) * COARSE]
    for k in range(0, depth, 128):
        at_ref[0:LANES, k : k + 128] = ah_ref[k : k + 128, :].T
        at_ref[LANES : 2 * LANES, k : k + 128] = al_ref[k : k + 128, :].T

    def sum_partners(i, carry):
        def add(place, total):
            j = list_ref[devices + 1 + place]
            scale = x_ref[j, ROWS : ROWS + 1, :].astype(jnp.float32)
            return total + x_ref[j, 0:ROWS, :].astype(jnp.float32) * scale

        total = lax.fori_loop(
            list_ref[i], list_ref[i + 1], add, jnp.zeros((ROWS, LANES), jnp.float32)
        )

        def put(u1, value):
            high, low = split(value)
            at = pl.multiple_of(((u1 + REACH) * devices + i) * COARSE, COARSE)
            yh_ref[pl.ds(at, COARSE), :] = high
            yl_ref[pl.ds(at, COARSE), :] = low

        for u1 in range(FINE):
            put(u1, total[u1 * COARSE : (u1 + 1) * COARSE])
        for u1 in range(REACH):
            put(u1 + FINE, pltpu.roll(total[u1 * COARSE : (u1 + 1) * COARSE], COARSE - 1, 0))
        for u1 in range(FINE - REACH, FINE):
            put(u1 - FINE, pltpu.roll(total[u1 * COARSE : (u1 + 1) * COARSE], 1, 0))
        return carry

    lax.fori_loop(0, devices, sum_partners, 0)
    products = []
    for j in range(SHIFTS):
        both = jnp.dot(
            at_ref[...], yh_ref[j * slab : j * slab + depth, :], preferred_element_type=jnp.float32
        )
        rest = jnp.dot(
            at_ref[0:LANES, :],
            yl_ref[j * slab : j * slab + depth, :],
            preferred_element_type=jnp.float32,
        )
        products.append(both[0:LANES] + both[LANES : 2 * LANES] + rest)
    product = jnp.concatenate(products, axis=1)
    stack = jnp.zeros((CH, OUT_LANES), jnp.float32)
    for v in range(STEP):
        stack = stack + product[CH * v : CH * (v + 1), CH * v : CH * v + OUT_LANES]
    count = list_ref[devices].astype(jnp.float32)
    stack = stack / jnp.sqrt(jnp.full((CH, OUT_LANES), count * span, jnp.float32))
    for a in range(CH):
        out_ref[0:1, a * OUT_LANES : (a + 1) * OUT_LANES] = stack[a : a + 1]


def stack_bin(devices, span, pairs, near, far):
    depth = devices * ROWS
    extended = devices * COARSE * (FINE + 2 * REACH)
    return pl.pallas_call(
        functools.partial(stack_kernel, devices, float(span)),
        out_shape=jax.ShapeDtypeStruct((1, CH * OUT_LANES), jnp.float32),
        in_specs=[SMEM, ANY, ANY],
        out_specs=VMEM,
        scratch_shapes=[
            pltpu.VMEM((devices, HEAD, LANES), jnp.bfloat16),
            pltpu.VMEM((depth, LANES), jnp.bfloat16),
            pltpu.VMEM((depth, LANES), jnp.bfloat16),
            pltpu.VMEM((2 * LANES, depth), jnp.bfloat16),
            pltpu.VMEM((extended, LANES), jnp.bfloat16),
            pltpu.VMEM((extended, LANES), jnp.bfloat16),
            pltpu.SemaphoreType.DMA((2,)),
        ],
        compiler_params=pltpu.CompilerParams(
            vmem_limit_bytes=(8 << 20) + devices * (5 << 18)
        ),
        name="stack",
    )(pairs, near, far)


def on_device(samples, scales, bin_ids, owner_table):
    devices = lax.axis_size("chan")
    span = samples.shape[1] - 2 * LAG
    own = lax.axis_index("chan").reshape(1).astype(jnp.int32)

    def swap(value, offset):
        return lax.ppermute(value, "chan", [(i, i ^ offset) for i in range(devices)])

    piece = prep(samples, scales)
    column = [piece] + [swap(piece, offset) for offset in range(4, devices, 4)]
    plane = column + [swap(one, 2) for one in column]
    near = jnp.stack(plane)
    far = swap(near, 1)
    pairs = find_pairs(devices, own, bin_ids, owner_table)
    return stack_bin(devices, span, pairs, near, far)


def solution(mesh):
    placed = (P(("groups", "chan"), None), P(("groups", "chan")), P(), P())
    return jax.shard_map(
        on_device,
        mesh=mesh,
        in_specs=placed,
        out_specs=P(("groups", "chan"), None),
        check_vma=False,
    )
```

time: 206 us -> 29.9 us (0.15)
  local copies, waits for them, and re-layouts: 68.5 us -> 2.2 us
  waiting for transfers between devices: 57.3 us -> 5.89 us
  blocking collectives: 35.1 us -> 0 us
  other arithmetic: 24.2 us -> 0 us
  between operations: 15.1 us -> 0.08 us
  Pallas kernels: 0 us -> 10.8 us
  starting transfers between devices: 0.04 us -> 10.6 us
  matrix products: 4.11 us -> 0 us
    another operation x70 -> x1, local copies, waits for them, and re-layouts: 62 us -> 0.01 us  [on_device(): near = jnp.stack(plane)]
    reduce_scatter x1 -> x0, waiting for transfers between devices: 56.5 us -> none  [on_device(): summed = lax.psum_scatter(running, 'chan', scatter_dimension=0, tiled=True)]
    unnamed x1 -> x0, blocking collectives: 35.1 us -> none
    scatter-add x1 -> x0, other arithmetic: 20.5 us -> none  [on_device(): initial.at[slot_ids, :, :, channel % per_dev]]
    pallas_call x0 -> x3, Pallas kernels: none -> 10.8 us  [the longest x1 7.65 us: stack_bin(): pl.pallas_call(functools.partial(stack_kernel, devices, float(span)), out...]
    ppermute x0 -> x8, starting transfers between devices: none -> 10.6 us  [swap(): lax.ppermute(value, 'chan', [(i, i ^ offset) for i in range(devices)])]
    ppermute x0 -> x8, waiting for transfers between devices: none -> 5.89 us  [swap(): lax.ppermute(value, 'chan', [(i, i ^ offset) for i in range(devices)])]
    dot_general x1 -> x0, matrix products: 4.11 us -> none  [on_device(): lax.dot_general(unfolded, record, (((1,), (1,)), ((), ())), preferred_ele...]
  transfers between devices with their start and end apart: 2 -> 8, of which waited for: 1 -> 3; matrix products, arithmetic and copies ran while one was open for 33% -> 0% of each run, Pallas kernels for 0% -> 8%
where the time goes in v1:
time: 29.9 us; the launch traced here: 29.7 us
  Pallas kernels  10.8 us (36%)
  starting transfers between devices  10.6 us (35%)
  waiting for transfers between devices  5.89 us (20%)
  local copies, waits for them, and re-layouts  2.2 us (7%)
    ppermute x8, starting transfers between devices, swap(): lax.ppermute(value, 'chan', [(i, i ^ offset) for i in range(devices)])  10.6 us
    pallas_call x1, Pallas kernels, stack_bin(): pl.pallas_call(functools.partial(stack_kernel, devices, float(span)), out...  7.65 us
    ppermute x8, waiting for transfers between devices, swap(): lax.ppermute(value, 'chan', [(i, i ^ offset) for i in range(devices)])  5.89 us
    pallas_call x1, Pallas kernels, find_pairs(): pl.pallas_call(functools.partial(pairs_kernel, devices), out_shape=jax.Sh...  2.47 us
    unnamed x15, local copies, waits for them, and re-layouts  2.19 us
    pallas_call x1, Pallas kernels, prep(): pl.pallas_call(prep_kernel, out_shape=jax.ShapeDtypeStruct((HEAD, LANES),...  0.72 us
  transfers between devices with their start and end apart: 8, of which 3 were waited for; matrix products, arithmetic and copies ran while one was open for 0% of the time, Pallas kernels for 8%

profile of v1, /device:TPU:0, one launch (start us, length us, event | category | flops | bytes accessed | tf_op | source)
XLA Modules:
  0.0 29.7 jit_solution(12650329747261300224)
XLA Ops:
  0.0 0.0 copy-start.2
  0.0 0.7 %copy-done.2 = bf16[16]{0:T(256)(128)(2,1)S(1)} copy-done((bf16[16]{0:T(256)(128)(2,1)S(1)}, bf16[16]{0:T(256)(128)(2,1)}, u32[]{:S(2)}) %copy-start.2) | copy-done | bytes 56
  0.7 0.0 copy-start
  0.7 0.8 %copy-done = bf16[16,2048]{1,0:T(8,128)(2,1)S(1)} copy-done((bf16[16,2048]{1,0:T(8,128)(2,1)S(1)}, bf16[16,2048]{1,0:T(8,128)(2,1)}, u32[]{:S(2)}) %copy-start) | copy-done | bytes 65560
  1.5 0.7 %prep.1 = bf16[136,256]{1,0:T(8,128)(2,1)S(1)} custom-call(bf16[16,2048]{1,0:T(8,128)(2,1)S(1)} %copy-done, bf16[1,16]{1,0:T(2,128)(2,1)S(1)} %bitcast.18), custom_call_target="tpu_custom_call" | custom-call | tf_op jit(solution)/shard_map/prep/pallas_call | solution.py:53
  2.2 3.1 %collective-permute-start = (bf16[136,256]{1,0:T(8,128)(2,1)S(1)}, bf16[136,256]{1,0:T(8,128)(2,1)S(1)}, u32[]{:S(2)}, u32[]{:S(2)}) collective-permute-start(bf16[136,256]{1,0:T(8,128)(2,1)S(1)} %prep.1), channel_id=1, source_target_pairs={{0,4},{1,5},{2,6},{3,7},{4,0},{5,1},{6,2},{7,3},{8,12},{9,13},{10,... | collective-permute-start | bytes 208904 | tf_op jit(solution)/shard_map/ppermute | solution.py:204
  5.3 2.6 %collective-permute-start.1 = (bf16[136,256]{1,0:T(8,128)(2,1)S(1)}, bf16[136,256]{1,0:T(8,128)(2,1)S(1)}, u32[]{:S(2)}, u32[]{:S(2)}) collective-permute-start(bf16[136,256]{1,0:T(8,128)(2,1)S(1)} %prep.1), channel_id=1, source_target_pairs={{0,8},{1,9},{2,10},{3,11},{4,12},{5,13},{6,14},{7,15},{8,0},{9,1},... | collective-permute-start | bytes 208904 | tf_op jit(solution)/shard_map/ppermute | solution.py:204
  7.9 0.0 collective-permute-start.2
  7.9 1.7 %collective-permute-start.3 = (bf16[136,256]{1,0:T(8,128)(2,1)S(1)}, bf16[136,256]{1,0:T(8,128)(2,1)S(1)}, u32[]{:S(2)}, u32[]{:S(2)}) collective-permute-start(bf16[136,256]{1,0:T(8,128)(2,1)S(1)} %prep.1), channel_id=1, source_target_pairs={{0,2},{1,3},{2,0},{3,1},{4,6},{5,7},{6,4},{7,5},{8,10},{9,11},{10,... | collective-permute-start | bytes 208904 | tf_op jit(solution)/shard_map/ppermute | solution.py:204
  9.7 0.0 collective-permute-done
  9.7 0.4 %collective-permute-start.4 = (bf16[136,256]{1,0:T(8,128)(2,1)S(1)}, bf16[136,256]{1,0:T(8,128)(2,1)S(1)}, u32[]{:S(2)}, u32[]{:S(2)}) collective-permute-start(bf16[136,256]{1,0:T(8,128)(2,1)S(1)} %collective-permute-done), channel_id=1, source_target_pairs={{0,2},{1,3},{2,0},{3,1},{4,6},{5,7},{6,4},{7,5},{8,10},{9,11},{10,... | collective-permute-start | bytes 208904 | tf_op jit(solution)/shard_map/ppermute | solution.py:204
  10.0 2.8 %collective-permute-done.1 = bf16[136,256]{1,0:T(8,128)(2,1)S(1)} collective-permute-done((bf16[136,256]{1,0:T(8,128)(2,1)S(1)}, bf16[136,256]{1,0:T(8,128)(2,1)S(1)}, u32[]{:S(2)}, u32[]{:S(2)}) %collective-permute-start.1) | collective-permute-done | bytes 69664 | tf_op jit(solution)/shard_map/ppermute | solution.py:204
  12.9 1.5 %collective-permute-start.5 = (bf16[136,256]{1,0:T(8,128)(2,1)S(1)}, bf16[136,256]{1,0:T(8,128)(2,1)S(1)}, u32[]{:S(2)}, u32[]{:S(2)}) collective-permute-start(bf16[136,256]{1,0:T(8,128)(2,1)S(1)} %collective-permute-done.1), channel_id=1, source_target_pairs={{0,2},{1,3},{2,0},{3,1},{4,6},{5,7},{6,4},{7,5},{8,10},{9,11},{10,... | collective-permute-start | bytes 208904 | tf_op jit(solution)/shard_map/ppermute | solution.py:204
  14.4 0.0 collective-permute-done.2
  14.4 1.3 %collective-permute-start.6 = (bf16[136,256]{1,0:T(8,128)(2,1)S(1)}, bf16[136,256]{1,0:T(8,128)(2,1)S(1)}, u32[]{:S(2)}, u32[]{:S(2)}) collective-permute-start(bf16[136,256]{1,0:T(8,128)(2,1)S(1)} %collective-permute-done.2), channel_id=1, source_target_pairs={{0,2},{1,3},{2,0},{3,1},{4,6},{5,7},{6,4},{7,5},{8,10},{9,11},{10,... | collective-permute-start | bytes 208904 | tf_op jit(solution)/shard_map/ppermute | solution.py:204
  15.7 0.0 collective-permute-done.3
  15.7 0.0 collective-permute-done.4
  15.7 1.5 %collective-permute-done.5 = bf16[136,256]{1,0:T(8,128)(2,1)S(1)} collective-permute-done((bf16[136,256]{1,0:T(8,128)(2,1)S(1)}, bf16[136,256]{1,0:T(8,128)(2,1)S(1)}, u32[]{:S(2)}, u32[]{:S(2)}) %collective-permute-start.5) | collective-permute-done | bytes 69664 | tf_op jit(solution)/shard_map/ppermute | solution.py:204
  17.2 1.6 %collective-permute-done.6 = bf16[136,256]{1,0:T(8,128)(2,1)S(1)} collective-permute-done((bf16[136,256]{1,0:T(8,128)(2,1)S(1)}, bf16[136,256]{1,0:T(8,128)(2,1)S(1)}, u32[]{:S(2)}, u32[]{:S(2)}) %collective-permute-start.6) | collective-permute-done | bytes 69664 | tf_op jit(solution)/shard_map/ppermute | solution.py:204
  18.8 0.0 copy-start.1
  18.8 0.1 collective-permute-start.7
  18.9 0.0 copy-start.3
  18.9 0.6 %copy-done.1 = s32[16,16]{1,0:T(8,128)S(1)} copy-done((s32[16,16]{1,0:T(8,128)S(1)}, s32[16,16]{1,0:T(8,128)}, u32[]{:S(2)}) %copy-start.1) | copy-done | bytes 1048
  19.5 0.1 copy-done.3
  19.5 2.5 %pairs.1.list_ref = s32[274]{0:T(512)S(1)} custom-call(s32[1]{0:T(128)} %bitcast.own_ref, s32[16,16]{1,0:T(8,128)S(1)} %copy-done.1, s32[16]{0:T(128)S(1)} %copy-done.3), custom_call_target="tpu_custom_call" | custom-call | tf_op jit(solution)/shard_map/pairs/pallas_call | solution.py:83
  22.0 0.0 collective-permute-done.7.far_ref
  22.0 7.6 %stack.37 = f32[1,16640]{1,0:T(1,128)} custom-call(s32[274]{0:T(512)S(1)} %pairs.1.list_ref, bf16[8,136,256]{2,1,0:T(8,128)(2,1)S(1)} %bitcast_dynamic-update-slice_fusion.near_ref, bf16[8,136,256]{2,1,0:T(8,128)(2,1)S(1)} %collective-permute-done.7.far_ref), custom_call_target="tpu_custom_call" | custom-call | tf_op jit(solution)/shard_map/stack/pallas_call | solution.py:177
  (8 shorter events, 0.0 us)
Async XLA Ops:
  0.0 0.7 %copy-start.2 = (bf16[16]{0:T(256)(128)(2,1)S(1)}, bf16[16]{0:T(256)(128)(2,1)}, u32[]{:S(2)}) copy-start(bf16[16]{0:T(256)(128)(2,1)} %param.5) | copy-start | bytes 100
  0.7 0.8 %copy-start = (bf16[16,2048]{1,0:T(8,128)(2,1)S(1)}, bf16[16,2048]{1,0:T(8,128)(2,1)}, u32[]{:S(2)}) copy-start(bf16[16,2048]{1,0:T(8,128)(2,1)} %samples_ref.1) | copy-start | bytes 196612
  2.2 7.5 %collective-permute-start = (bf16[136,256]{1,0:T(8,128)(2,1)S(1)}, bf16[136,256]{1,0:T(8,128)(2,1)S(1)}, u32[]{:S(2)}, u32[]{:S(2)}) collective-permute-start(bf16[136,256]{1,0:T(8,128)(2,1)S(1)} %prep.1), channel_id=1, source_target_pairs={{0,4},{1,5},{2,6},{3,7},{4,0},{5,1},{6,2},{7,3},{8,12},{9,13},{10,... | collective-permute-start | bytes 208904 | tf_op jit(solution)/shard_map/ppermute | solution.py:204
  5.3 7.5 %collective-permute-start.1 = (bf16[136,256]{1,0:T(8,128)(2,1)S(1)}, bf16[136,256]{1,0:T(8,128)(2,1)S(1)}, u32[]{:S(2)}, u32[]{:S(2)}) collective-permute-start(bf16[136,256]{1,0:T(8,128)(2,1)S(1)} %prep.1), channel_id=1, source_target_pairs={{0,8},{1,9},{2,10},{3,11},{4,12},{5,13},{6,14},{7,15},{8,0},{9,1},... | collective-permute-start | bytes 208904 | tf_op jit(solution)/shard_map/ppermute | solution.py:204
  7.9 6.5 %collective-permute-start.2 = (bf16[136,256]{1,0:T(8,128)(2,1)S(1)}, bf16[136,256]{1,0:T(8,128)(2,1)S(1)}, u32[]{:S(2)}, u32[]{:S(2)}) collective-permute-start(bf16[136,256]{1,0:T(8,128)(2,1)S(1)} %prep.1), channel_id=1, source_target_pairs={{0,12},{1,13},{2,14},{3,15},{4,8},{5,9},{6,10},{7,11},{8,4},{9,5},... | collective-permute-start | bytes 208904 | tf_op jit(solution)/shard_map/ppermute | solution.py:204
  7.9 7.7 %collective-permute-start.3 = (bf16[136,256]{1,0:T(8,128)(2,1)S(1)}, bf16[136,256]{1,0:T(8,128)(2,1)S(1)}, u32[]{:S(2)}, u32[]{:S(2)}) collective-permute-start(bf16[136,256]{1,0:T(8,128)(2,1)S(1)} %prep.1), channel_id=1, source_target_pairs={{0,2},{1,3},{2,0},{3,1},{4,6},{5,7},{6,4},{7,5},{8,10},{9,11},{10,... | collective-permute-start | bytes 208904 | tf_op jit(solution)/shard_map/ppermute | solution.py:204
  9.7 6.0 %collective-permute-start.4 = (bf16[136,256]{1,0:T(8,128)(2,1)S(1)}, bf16[136,256]{1,0:T(8,128)(2,1)S(1)}, u32[]{:S(2)}, u32[]{:S(2)}) collective-permute-start(bf16[136,256]{1,0:T(8,128)(2,1)S(1)} %collective-permute-done), channel_id=1, source_target_pairs={{0,2},{1,3},{2,0},{3,1},{4,6},{5,7},{6,4},{7,5},{8,10},{9,11},{10,... | collective-permute-start | bytes 208904 | tf_op jit(solution)/shard_map/ppermute | solution.py:204
  12.9 4.3 %collective-permute-start.5 = (bf16[136,256]{1,0:T(8,128)(2,1)S(1)}, bf16[136,256]{1,0:T(8,128)(2,1)S(1)}, u32[]{:S(2)}, u32[]{:S(2)}) collective-permute-start(bf16[136,256]{1,0:T(8,128)(2,1)S(1)} %collective-permute-done.1), channel_id=1, source_target_pairs={{0,2},{1,3},{2,0},{3,1},{4,6},{5,7},{6,4},{7,5},{8,10},{9,11},{10,... | collective-permute-start | bytes 208904 | tf_op jit(solution)/shard_map/ppermute | solution.py:204
  14.4 4.4 %collective-permute-start.6 = (bf16[136,256]{1,0:T(8,128)(2,1)S(1)}, bf16[136,256]{1,0:T(8,128)(2,1)S(1)}, u32[]{:S(2)}, u32[]{:S(2)}) collective-permute-start(bf16[136,256]{1,0:T(8,128)(2,1)S(1)} %collective-permute-done.2), channel_id=1, source_target_pairs={{0,2},{1,3},{2,0},{3,1},{4,6},{5,7},{6,4},{7,5},{8,10},{9,11},{10,... | collective-permute-start | bytes 208904 | tf_op jit(solution)/shard_map/ppermute | solution.py:204
  18.8 0.7 %copy-start.1 = (s32[16,16]{1,0:T(8,128)S(1)}, s32[16,16]{1,0:T(8,128)}, u32[]{:S(2)}) copy-start(s32[16,16]{1,0:T(8,128)} %bins_ref.1) | copy-start | bytes 3076
  18.8 3.2 %collective-permute-start.7 = (bf16[8,136,256]{2,1,0:T(8,128)(2,1)S(1)}, bf16[8,136,256]{2,1,0:T(8,128)(2,1)S(1)}, u32[]{:S(2)}, u32[]{:S(2)}) collective-permute-start(bf16[8,136,256]{2,1,0:T(8,128)(2,1)S(1)} %bitcast_dynamic-update-slice_fusion.near_ref), channel_id=1, source_target_pairs={{0,1},{1,0},{2,3},{3,2},{4,5},{5,4},{6,7},{7,6},{8,9},{9,8},{10,11... | collective-permute-start | bytes 1671176 | tf_op jit(solution)/shard_map/ppermute | solution.py:204
  18.9 0.7 %copy-start.3 = (s32[16]{0:T(128)S(1)}, s32[16]{0:T(128)}, u32[]{:S(2)}) copy-start(s32[16]{0:T(128)} %owner_ref.1) | copy-start | bytes 196

commit v2 on v1

v2 whole, which is shorter than its diff:
```python
import functools

import jax
import jax.numpy as jnp
from jax import lax
from jax.experimental import pallas as pl
from jax.experimental.pallas import tpu as pltpu
from jax.sharding import PartitionSpec as P

LAG = 32
LAGS = 65
CH = 16
STEP = 16
LANES = CH * STEP
FINE = 8
COARSE = 16
ROWS = FINE * COARSE
HEAD = ROWS + 8
REACH = LAG // STEP
SHIFTS = 2 * REACH + 1
OUT_LANES = LAGS * CH
GROUPS = 4

VMEM = pl.BlockSpec(memory_space=pltpu.VMEM)
SMEM = pl.BlockSpec(memory_space=pltpu.SMEM)
ANY = pl.BlockSpec(memory_space=pl.ANY)
HBM = pl.BlockSpec(memory_space=pltpu.HBM)


def piece_offset(devices, index):
    far = devices // GROUPS
    return (
        lax.rem(index, far) * 4 + lax.rem(lax.div(index, far), 2) * 2 + lax.div(index, 2 * far)
    )


def prep_kernel(samples_ref, scales_ref, piece_ref, x_ref, s_ref, turned_ref, sem):
    copies = [
        pltpu.make_async_copy(samples_ref, x_ref, sem.at[0]),
        pltpu.make_async_copy(scales_ref, s_ref, sem.at[1]),
    ]
    for copy in copies:
        copy.start()
    copies[0].wait()
    samples = x_ref[...].astype(jnp.float32)
    for u2 in range(COARSE):
        turned_ref[u2 * 128 : (u2 + 1) * 128, 0:CH] = samples[:, u2 * 128 : (u2 + 1) * 128].T
    for u1 in range(FINE):
        parts = [
            turned_ref[pl.ds(STEP * u1 + v, COARSE, stride=128), 0:CH] for v in range(STEP)
        ]
        piece_ref[u1 * COARSE : (u1 + 1) * COARSE, :] = jnp.concatenate(parts, axis=1).astype(
            jnp.bfloat16
        )
    copies[1].wait()
    scales = s_ref[...].astype(jnp.float32)
    piece_ref[ROWS:HEAD, :] = jnp.broadcast_to(
        jnp.concatenate([scales] * STEP, axis=1), (HEAD - ROWS, LANES)
    ).astype(jnp.bfloat16)


def prep(samples, scales):
    return pl.pallas_call(
        prep_kernel,
        out_shape=jax.ShapeDtypeStruct((HEAD, LANES), jnp.bfloat16),
        in_specs=[HBM, HBM],
        out_specs=VMEM,
        scratch_shapes=[
            pltpu.VMEM(samples.shape, jnp.bfloat16),
            pltpu.VMEM((1, CH), jnp.bfloat16),
            pltpu.VMEM((COARSE * 128, 128), jnp.float32),
            pltpu.SemaphoreType.DMA((2,)),
        ],
        compiler_params=pltpu.CompilerParams(vmem_limit_bytes=4 << 20),
        name="prep",
    )(
        pltpu.with_memory_space_constraint(samples, pltpu.HBM),
        pltpu.with_memory_space_constraint(scales.reshape(1, CH), pltpu.HBM),
    )


def pairs_kernel(devices, own_ref, bins_ref, owner_ref, list_ref):
    own = own_ref[0]
    early_at, late_at = 2, 3 + devices * devices
    first_late = devices - devices // GROUPS
    own_bin = jnp.int32(0)
    for i in range(devices):
        own_bin = jnp.where(owner_ref[i] == own, i, own_bin)

    def row(i, found):
        early, late = found
        p = own ^ piece_offset(devices, i)
        for j in range(devices):
            q = own ^ piece_offset(devices, jnp.int32(j))
            hit = jnp.where(bins_ref[p, q] == own_bin, 1, 0)
            code = i * devices + j
            if j < first_late:
                list_ref[early_at + early] = code
                early = early + hit
            else:
                list_ref[late_at + late] = code
                late = late + hit
        return early, late

    early, late = lax.fori_loop(0, devices, row, (jnp.int32(0), jnp.int32(0)))
    list_ref[0] = early
    list_ref[1] = late


def find_pairs(devices, own, bin_ids, owner_table):
    return pl.pallas_call(
        functools.partial(pairs_kernel, devices),
        out_shape=jax.ShapeDtypeStruct((2 * devices * devices + 4,), jnp.int32),
        in_specs=[SMEM] * 3,
        out_specs=SMEM,
        compiler_params=pltpu.CompilerParams(vmem_limit_bytes=1 << 20),
        cost_estimate=pl.CostEstimate(flops=10_000_000, bytes_accessed=1 << 20, transcendentals=0),
        name="pairs",
    )(own, bin_ids, owner_table)


def split(value):
    high = value.astype(jnp.bfloat16)
    return high, (value - high.astype(jnp.float32)).astype(jnp.bfloat16)


def inside_rows():
    row = lax.broadcasted_iota(jnp.int32, (ROWS, LANES), 0)
    u = FINE * (row % COARSE) + row // COARSE
    return (u >= REACH) & (u < ROWS - REACH)


def turn_group(load, members, turned_ref, high_ref, low_ref):
    inside = inside_rows()
    for i in range(members):
        scale = load(i, ROWS, ROWS + 1)
        high, low = split(jnp.where(inside, load(i, 0, ROWS) * scale, 0.0))
        for u1 in range(FINE):
            at = (u1 * members + i) * COARSE
            high_ref[at : at + COARSE, :] = high[u1 * COARSE : (u1 + 1) * COARSE]
            low_ref[at : at + COARSE, :] = low[u1 * COARSE : (u1 + 1) * COARSE]
    for k in range(0, members * ROWS, 128):
        turned_ref[0:LANES, k : k + 128] = high_ref[k : k + 128, :].T
        turned_ref[LANES : 2 * LANES, k : k + 128] = low_ref[k : k + 128, :].T


def loader(ref):
    return lambda i, start, stop: ref[i, start:stop, :].astype(jnp.float32)


def turn_kernel(x_hbm, turned_ref, x_ref, high_ref, low_ref, sem):
    copy = pltpu.make_async_copy(x_hbm, x_ref, sem)
    copy.start()
    copy.wait()
    turn_group(loader(x_ref), x_ref.shape[0], turned_ref, high_ref, low_ref)


def turn(pieces):
    members = pieces.shape[0]
    return pl.pallas_call(
        turn_kernel,
        out_shape=jax.ShapeDtypeStruct((2 * LANES, members * ROWS), jnp.bfloat16),
        in_specs=[ANY],
        out_specs=VMEM,
        scratch_shapes=[
            pltpu.VMEM(pieces.shape, jnp.bfloat16),
            pltpu.VMEM((members * ROWS, LANES), jnp.bfloat16),
            pltpu.VMEM((members * ROWS, LANES), jnp.bfloat16),
            pltpu.SemaphoreType.DMA,
        ],
        compiler_params=pltpu.CompilerParams(vmem_limit_bytes=(2 << 20) + members * (1 << 19)),
        cost_estimate=pl.CostEstimate(
            flops=members * 2_000_000, bytes_accessed=members << 18, transcendentals=0
        ),
        name="turn",
    )(pieces)


def add_pairs(devices, first, base, count, list_ref, x_ref, sums_ref):
    def add(place, carry):
        code = list_ref[base + place]
        i, j = lax.div(code, devices), lax.rem(code, devices) - first
        scale = x_ref[j, ROWS : ROWS + 1, :].astype(jnp.float32)
        sums_ref[i] = sums_ref[i] + x_ref[j, 0:ROWS, :].astype(jnp.float32) * scale
        return carry

    lax.fori_loop(0, count, add, 0)


def middle_kernel(devices, list_ref, near_hbm, side_hbm, turned_y_ref, turned_s_ref, sums_ref, x_ref, high_ref, low_ref, sem):
    members = devices // GROUPS
    copies = [
        pltpu.make_async_copy(near_hbm, x_ref.at[pl.ds(0, 2 * members)], sem.at[0]),
        pltpu.make_async_copy(side_hbm, x_ref.at[pl.ds(2 * members, members)], sem.at[1]),
    ]
    for copy in copies:
        copy.start()
    sums_ref[...] = jnp.zeros_like(sums_ref)
    for copy in copies:
        copy.wait()
    for turned_ref, base in ((turned_y_ref, members), (turned_s_ref, 2 * members)):
        turn_group(
            lambda i, a, b, base=base: x_ref[base + i, a:b, :].astype(jnp.float32),
            members,
            turned_ref,
            high_ref,
            low_ref,
        )
    add_pairs(devices, 0, 2, list_ref[0], list_ref, x_ref, sums_ref)


def middle(devices, pairs, near, side):
    members = devices // GROUPS
    turned = jax.ShapeDtypeStruct((2 * LANES, members * ROWS), jnp.bfloat16)
    return pl.pallas_call(
        functools.partial(middle_kernel, devices),
        out_shape=(turned, turned, jax.ShapeDtypeStruct((devices, ROWS, LANES), jnp.float32)),
        in_specs=[SMEM, ANY, ANY],
        out_specs=(VMEM, VMEM, VMEM),
        scratch_shapes=[
            pltpu.VMEM((3 * members, HEAD, LANES), jnp.bfloat16),
            pltpu.VMEM((members * ROWS, LANES), jnp.bfloat16),
            pltpu.VMEM((members * ROWS, LANES), jnp.bfloat16),
            pltpu.SemaphoreType.DMA((2,)),
        ],
        compiler_params=pltpu.CompilerParams(vmem_limit_bytes=(2 << 20) + devices * (1 << 19)),
        cost_estimate=pl.CostEstimate(
            flops=devices * 2_000_000, bytes_accessed=devices << 18, transcendentals=0
        ),
        name="middle",
    )(pairs, near, side)


def stack_kernel(
    devices, span, list_ref, t0_ref, t1_ref, t2_ref, sums_hbm, last_hbm, out_ref,
    x_ref, sums_ref, a0_ref, a1_ref, a2_ref, a3_ref, high_ref, low_ref, yh_ref, yl_ref, sem,
):
    members = devices // GROUPS
    depth = members * ROWS
    slab = members * COARSE
    copies = [
        pltpu.make_async_copy(last_hbm, x_ref, sem.at[0]),
        pltpu.make_async_copy(sums_hbm, sums_ref, sem.at[1]),
        pltpu.make_async_copy(t0_ref, a0_ref, sem.at[2]),
        pltpu.make_async_copy(t1_ref, a1_ref, sem.at[3]),
        pltpu.make_async_copy(t2_ref, a2_ref, sem.at[4]),
    ]
    for copy in copies:
        copy.start()
    copies[0].wait()
    copies[1].wait()
    late_at = 3 + devices * devices
    add_pairs(devices, 3 * members, late_at, list_ref[1], list_ref, x_ref, sums_ref)
    for copy in copies[2:]:
        copy.wait()
    turn_group(loader(x_ref), members, a3_ref, high_ref, low_ref)

    def put(group, member, u1, value):
        high, low = split(value)
        at = ((u1 + REACH) * members + member) * COARSE
        yh_ref[group, at : at + COARSE, :] = high
        yl_ref[group, at : at + COARSE, :] = low

    products = [None] * SHIFTS
    for group, turned_ref in enumerate((a0_ref, a1_ref, a2_ref, a3_ref)):
        for member in range(members):
            total = sums_ref[group * members + member]
            parts = [total[u1 * COARSE : (u1 + 1) * COARSE] for u1 in range(FINE)]
            for u1 in range(FINE):
                put(group, member, u1, parts[u1])
            for u1 in range(REACH):
                put(group, member, u1 + FINE, pltpu.roll(parts[u1], COARSE - 1, 0))
            for u1 in range(FINE - REACH, FINE):
                put(group, member, u1 - FINE, pltpu.roll(parts[u1], 1, 0))
        for j in range(SHIFTS):
            both = jnp.dot(
                turned_ref[...],
                yh_ref[group, j * slab : j * slab + depth, :],
                preferred_element_type=jnp.float32,
            )
            rest = jnp.dot(
                turned_ref[0:LANES, :],
                yl_ref[group, j * slab : j * slab + depth, :],
                preferred_element_type=jnp.float32,
            )
            part = both[0:LANES] + both[LANES : 2 * LANES] + rest
            products[j] = part if group == 0 else products[j] + part
    product = jnp.concatenate(products, axis=1)
    stack = jnp.zeros((CH, OUT_LANES), jnp.float32)
    for v in range(STEP):
        stack = stack + product[CH * v : CH * (v + 1), CH * v : CH * v + OUT_LANES]
    count = (list_ref[0] + list_ref[1]).astype(jnp.float32)
    stack = stack / jnp.sqrt(jnp.full((CH, OUT_LANES), count * span, jnp.float32))
    for a in range(CH):
        out_ref[0:1, a * OUT_LANES : (a + 1) * OUT_LANES] = stack[a : a + 1]


def stack_bin(devices, span, pairs, turned, sums, last):
    members = devices // GROUPS
    depth = members * ROWS
    extended = members * COARSE * (FINE + 2 * REACH)
    left = pltpu.VMEM((2 * LANES, depth), jnp.bfloat16)
    return pl.pallas_call(
        functools.partial(stack_kernel, devices, float(span)),
        out_shape=jax.ShapeDtypeStruct((1, CH * OUT_LANES), jnp.float32),
        in_specs=[SMEM] + [ANY] * 5,
        out_specs=VMEM,
        scratch_shapes=[
            pltpu.VMEM((members, HEAD, LANES), jnp.bfloat16),
            pltpu.VMEM((devices, ROWS, LANES), jnp.float32),
            left,
            left,
            left,
            left,
            pltpu.VMEM((depth, LANES), jnp.bfloat16),
            pltpu.VMEM((depth, LANES), jnp.bfloat16),
            pltpu.VMEM((GROUPS, extended, LANES), jnp.bfloat16),
            pltpu.VMEM((GROUPS, extended, LANES), jnp.bfloat16),
            pltpu.SemaphoreType.DMA((5,)),
        ],
        compiler_params=pltpu.CompilerParams(vmem_limit_bytes=(8 << 20) + devices * (5 << 17)),
        name="stack",
    )(pairs, *turned, sums, last)


def on_device(samples, scales, bin_ids, owner_table):
    devices = lax.axis_size("chan")
    span = samples.shape[1] - 2 * LAG
    own = lax.axis_index("chan").reshape(1).astype(jnp.int32)

    def swap(value, offset):
        return lax.ppermute(value, "chan", [(i, i ^ offset) for i in range(devices)])

    piece = prep(samples, scales)
    pairs = find_pairs(devices, own, bin_ids, owner_table)
    members = devices // GROUPS
    near = jnp.zeros((2 * members,) + piece.shape, piece.dtype)
    near = near.at[0].set(piece)
    column = [piece]
    plane = [swap(piece, 2)]
    for i in range(1, members):
        one = swap(piece, 4 * i)
        column.append(one)
        plane.append(swap(one, 2))
        near = near.at[i].set(one)
    for i, one in enumerate(plane):
        near = near.at[members + i].set(one)
    own_column = jnp.stack(column)
    side_column = swap(own_column, 1)
    side_plane = swap(jnp.stack(plane), 1)
    turned_0 = turn(own_column)
    turned_1, turned_2, sums = middle(devices, pairs, near, side_column)
    return stack_bin(
        devices, span, pairs, (turned_0, turned_1, turned_2), sums, side_plane
    )


def solution(mesh):
    placed = (P(("groups", "chan"), None), P(("groups", "chan")), P(), P())
    return jax.shard_map(
        on_device,
        mesh=mesh,
        in_specs=placed,
        out_specs=P(("groups", "chan"), None),
        check_vma=False,
    )
```

time: 29.9 us -> 29.2 us (0.977)
  waiting for transfers between devices: 5.89 us -> 4.39 us
  Pallas kernels: 10.8 us -> 11.8 us
  local copies, waits for them, and re-layouts: 2.2 us -> 1.43 us
  starting transfers between devices: 10.6 us -> 11.2 us
    pallas_call x1, Pallas kernels: 7.65 us -> 6.07 us  [stack_bin(): pl.pallas_call(functools.partial(stack_kernel, devices, float(span)), out...]
    pallas_call x0 -> x2, Pallas kernels: none -> 1.56 us  [the longest x1 1.31 us: middle(): pl.pallas_call(functools.partial(middle_kernel, devices), out_shape=(turn...]
    ppermute x8 -> x9, waiting for transfers between devices: 5.89 us -> 4.39 us  [swap(): lax.ppermute(value, 'chan', [(i, i ^ offset) for i in range(devices)])]
    pallas_call x1, Pallas kernels: 0.72 us -> 1.66 us  [prep(): pl.pallas_call(prep_kernel, out_shape=jax.ShapeDtypeStruct((HEAD, LANES),...]
    unnamed x15 -> x4, local copies, waits for them, and re-layouts: 2.19 us -> 1.35 us
    ppermute x8 -> x9, starting transfers between devices: 10.6 us -> 11.2 us  [swap(): lax.ppermute(value, 'chan', [(i, i ^ offset) for i in range(devices)])]
  transfers between devices with their start and end apart: 8 -> 9, of which waited for: 3 -> 5; matrix products, arithmetic and copies ran while one was open for 0% -> 1% of each run, Pallas kernels for 8% -> 14%
where the time goes in v2:
time: 29.2 us; the launch traced here: 29 us
  Pallas kernels  11.8 us (40%)
  starting transfers between devices  11.2 us (38%)
  waiting for transfers between devices  4.39 us (15%)
  local copies, waits for them, and re-layouts  1.43 us (5%)
    ppermute x9, starting transfers between devices, swap(): lax.ppermute(value, 'chan', [(i, i ^ offset) for i in range(devices)])  11.2 us
    pallas_call x1, Pallas kernels, stack_bin(): pl.pallas_call(functools.partial(stack_kernel, devices, float(span)), out...  6.07 us
    ppermute x9, waiting for transfers between devices, swap(): lax.ppermute(value, 'chan', [(i, i ^ offset) for i in range(devices)])  4.39 us
    pallas_call x1, Pallas kernels, find_pairs(): pl.pallas_call(functools.partial(pairs_kernel, devices), out_shape=jax.Sh...  2.48 us
    pallas_call x1, Pallas kernels, prep(): pl.pallas_call(prep_kernel, out_shape=jax.ShapeDtypeStruct((HEAD, LANES),...  1.66 us
    unnamed x4, local copies, waits for them, and re-layouts  1.35 us
    pallas_call x1, Pallas kernels, middle(): pl.pallas_call(functools.partial(middle_kernel, devices), out_shape=(turn...  1.31 us
  transfers between devices with their start and end apart: 9, of which 5 were waited for; matrix products, arithmetic and copies ran while one was open for 1% of the time, Pallas kernels for 14%

profile of v2, /device:TPU:0, one launch (start us, length us, event | category | flops | bytes accessed | tf_op | source)
XLA Modules:
  0.0 29.0 jit_solution(3009546500689337763)
XLA Ops:
  0.0 1.7 %prep.1 = bf16[136,256]{1,0:T(8,128)(2,1)S(1)} custom-call(bf16[16,2048]{1,0:T(8,128)(2,1)} %samples_ref.1, bf16[1,16]{1,0:T(2,128)(2,1)} %bitcast.26), custom_call_target="tpu_custom_call" | custom-call | tf_op jit(solution)/shard_map/prep/pallas_call | solution.py:63
  1.7 3.1 %collective-permute-start = (bf16[136,256]{1,0:T(8,128)(2,1)S(1)}, bf16[136,256]{1,0:T(8,128)(2,1)S(1)}, u32[]{:S(2)}, u32[]{:S(2)}) collective-permute-start(bf16[136,256]{1,0:T(8,128)(2,1)S(1)} %prep.1), channel_id=1, source_target_pairs={{0,4},{1,5},{2,6},{3,7},{4,0},{5,1},{6,2},{7,3},{8,12},{9,13},{10,... | collective-permute-start | bytes 208904 | tf_op jit(solution)/shard_map/ppermute | solution.py:332
  4.8 2.6 %collective-permute-start.1 = (bf16[136,256]{1,0:T(8,128)(2,1)S(1)}, bf16[136,256]{1,0:T(8,128)(2,1)S(1)}, u32[]{:S(2)}, u32[]{:S(2)}) collective-permute-start(bf16[136,256]{1,0:T(8,128)(2,1)S(1)} %prep.1), channel_id=1, source_target_pairs={{0,8},{1,9},{2,10},{3,11},{4,12},{5,13},{6,14},{7,15},{8,0},{9,1},... | collective-permute-start | bytes 208904 | tf_op jit(solution)/shard_map/ppermute | solution.py:332
  7.4 0.0 collective-permute-start.2
  7.4 1.7 %collective-permute-start.3 = (bf16[136,256]{1,0:T(8,128)(2,1)S(1)}, bf16[136,256]{1,0:T(8,128)(2,1)S(1)}, u32[]{:S(2)}, u32[]{:S(2)}) collective-permute-start(bf16[136,256]{1,0:T(8,128)(2,1)S(1)} %prep.1), channel_id=1, source_target_pairs={{0,2},{1,3},{2,0},{3,1},{4,6},{5,7},{6,4},{7,5},{8,10},{9,11},{10,... | collective-permute-start | bytes 208904 | tf_op jit(solution)/shard_map/ppermute | solution.py:332
  9.2 0.0 copy-start
  9.2 0.7 %copy-done = s32[16,16]{1,0:T(8,128)S(1)} copy-done((s32[16,16]{1,0:T(8,128)S(1)}, s32[16,16]{1,0:T(8,128)}, u32[]{:S(2)}) %copy-start) | copy-done | bytes 1048
  9.9 0.0 copy-start.1
  9.9 0.7 %copy-done.1 = s32[16]{0:T(128)S(1)} copy-done((s32[16]{0:T(128)S(1)}, s32[16]{0:T(128)}, u32[]{:S(2)}) %copy-start.1) | copy-done | bytes 88
  10.5 2.5 %pairs.1.list_ref = s32[516]{0:T(1024)S(1)} custom-call(s32[1]{0:T(128)} %bitcast.own_ref, s32[16,16]{1,0:T(8,128)S(1)} %copy-done, s32[16]{0:T(128)S(1)} %copy-done.1), custom_call_target="tpu_custom_call" | custom-call | flops 10000000 | bytes 1048576 | tf_op jit(solution)/shard_map/pairs/pallas_call | solution.py:111
  13.0 0.0 collective-permute-done
  13.0 0.0 collective-permute-done.1
  13.0 0.6 %collective-permute-done.2 = bf16[136,256]{1,0:T(8,128)(2,1)S(1)} collective-permute-done((bf16[136,256]{1,0:T(8,128)(2,1)S(1)}, bf16[136,256]{1,0:T(8,128)(2,1)S(1)}, u32[]{:S(2)}, u32[]{:S(2)}) %collective-permute-start.2) | collective-permute-done | bytes 69664 | tf_op jit(solution)/shard_map/ppermute | solution.py:332
  13.6 0.1 collective-permute-start.7
  13.7 1.6 %collective-permute-start.4 = (bf16[136,256]{1,0:T(8,128)(2,1)S(1)}, bf16[136,256]{1,0:T(8,128)(2,1)S(1)}, u32[]{:S(2)}, u32[]{:S(2)}) collective-permute-start(bf16[136,256]{1,0:T(8,128)(2,1)S(1)} %collective-permute-done), channel_id=1, source_target_pairs={{0,2},{1,3},{2,0},{3,1},{4,6},{5,7},{6,4},{7,5},{8,10},{9,11},{10,... | collective-permute-start | bytes 208904 | tf_op jit(solution)/shard_map/ppermute | solution.py:332
  15.3 0.5 %collective-permute-start.5 = (bf16[136,256]{1,0:T(8,128)(2,1)S(1)}, bf16[136,256]{1,0:T(8,128)(2,1)S(1)}, u32[]{:S(2)}, u32[]{:S(2)}) collective-permute-start(bf16[136,256]{1,0:T(8,128)(2,1)S(1)} %collective-permute-done.1), channel_id=1, source_target_pairs={{0,2},{1,3},{2,0},{3,1},{4,6},{5,7},{6,4},{7,5},{8,10},{9,11},{10,... | collective-permute-start | bytes 208904 | tf_op jit(solution)/shard_map/ppermute | solution.py:332
  15.8 1.5 %collective-permute-start.6 = (bf16[136,256]{1,0:T(8,128)(2,1)S(1)}, bf16[136,256]{1,0:T(8,128)(2,1)S(1)}, u32[]{:S(2)}, u32[]{:S(2)}) collective-permute-start(bf16[136,256]{1,0:T(8,128)(2,1)S(1)} %collective-permute-done.2), channel_id=1, source_target_pairs={{0,2},{1,3},{2,0},{3,1},{4,6},{5,7},{6,4},{7,5},{8,10},{9,11},{10,... | collective-permute-start | bytes 208904 | tf_op jit(solution)/shard_map/ppermute | solution.py:332
  17.3 0.0 collective-permute-done.3
  17.4 0.2 turn.1.t0_ref
  17.6 0.9 %collective-permute-done.4 = bf16[136,256]{1,0:T(8,128)(2,1)S(1)} collective-permute-done((bf16[136,256]{1,0:T(8,128)(2,1)S(1)}, bf16[136,256]{1,0:T(8,128)(2,1)S(1)}, u32[]{:S(2)}, u32[]{:S(2)}) %collective-permute-start.4) | collective-permute-done | bytes 69664 | tf_op jit(solution)/shard_map/ppermute | solution.py:332
  18.5 1.8 %collective-permute-done.5 = bf16[136,256]{1,0:T(8,128)(2,1)S(1)} collective-permute-done((bf16[136,256]{1,0:T(8,128)(2,1)S(1)}, bf16[136,256]{1,0:T(8,128)(2,1)S(1)}, u32[]{:S(2)}, u32[]{:S(2)}) %collective-permute-start.5) | collective-permute-done | bytes 69664 | tf_op jit(solution)/shard_map/ppermute | solution.py:332
  20.3 0.9 %collective-permute-done.6 = bf16[136,256]{1,0:T(8,128)(2,1)S(1)} collective-permute-done((bf16[136,256]{1,0:T(8,128)(2,1)S(1)}, bf16[136,256]{1,0:T(8,128)(2,1)S(1)}, u32[]{:S(2)}, u32[]{:S(2)}) %collective-permute-start.6) | collective-permute-done | bytes 69664 | tf_op jit(solution)/shard_map/ppermute | solution.py:332
  21.3 0.1 collective-permute-start.8
  21.4 0.0 collective-permute-done.7.side_hbm
  21.4 1.3 %middle.1 = (bf16[512,512]{1,0:T(8,128)(2,1)S(1)}, bf16[512,512]{1,0:T(8,128)(2,1)S(1)}, f32[16,128,256]{2,1,0:T(8,128)S(1)}) custom-call(s32[516]{0:T(1024)S(1)} %pairs.1.list_ref, bf16[8,136,256]{2,1,0:T(8,128)(2,1)S(1)} %constant_dynamic-update-slice_fusion.near_hbm, bf16[4,136,256]{2,1,0:T(8,128)(2,1)S(1)} %collective-permute-done.7.side_hbm), custom_call_target="tpu_custom_call" | custom-call | flops 32000000 | bytes 4194304 | tf_op jit(solution)/shard_map/middle/pallas_call | solution.py:215
  22.8 0.2 collective-permute-done.8.last_hbm
  22.9 6.1 %stack.29 = f32[1,16640]{1,0:T(1,128)} custom-call(s32[516]{0:T(1024)S(1)} %pairs.1.list_ref, bf16[512,512]{1,0:T(8,128)(2,1)S(1)} %turn.1.t0_ref, bf16[512,512]{1,0:T(8,128)(2,1)S(1)} %get-tuple-element.104.t1_ref, bf16[512,512]{1,0:T(8,128)(2,1)S(1)} %get-tuple-element.105.t2_ref, f32[16,128,256]{2,1,0:T(8,128)S(1)} %get-tuple-element.106.sums_hbm, ...), custom_call_target="tpu_custom_call" | custom-call | tf_op jit(solution)/shard_map/stack/pallas_call | solution.py:303
  (10 shorter events, 0.2 us)
Async XLA Ops:
  1.7 11.3 %collective-permute-start = (bf16[136,256]{1,0:T(8,128)(2,1)S(1)}, bf16[136,256]{1,0:T(8,128)(2,1)S(1)}, u32[]{:S(2)}, u32[]{:S(2)}) collective-permute-start(bf16[136,256]{1,0:T(8,128)(2,1)S(1)} %prep.1), channel_id=1, source_target_pairs={{0,4},{1,5},{2,6},{3,7},{4,0},{5,1},{6,2},{7,3},{8,12},{9,13},{10,... | collective-permute-start | bytes 208904 | tf_op jit(solution)/shard_map/ppermute | solution.py:332
  4.8 8.2 %collective-permute-start.1 = (bf16[136,256]{1,0:T(8,128)(2,1)S(1)}, bf16[136,256]{1,0:T(8,128)(2,1)S(1)}, u32[]{:S(2)}, u32[]{:S(2)}) collective-permute-start(bf16[136,256]{1,0:T(8,128)(2,1)S(1)} %prep.1), channel_id=1, source_target_pairs={{0,8},{1,9},{2,10},{3,11},{4,12},{5,13},{6,14},{7,15},{8,0},{9,1},... | collective-permute-start | bytes 208904 | tf_op jit(solution)/shard_map/ppermute | solution.py:332
  7.4 6.2 %collective-permute-start.2 = (bf16[136,256]{1,0:T(8,128)(2,1)S(1)}, bf16[136,256]{1,0:T(8,128)(2,1)S(1)}, u32[]{:S(2)}, u32[]{:S(2)}) collective-permute-start(bf16[136,256]{1,0:T(8,128)(2,1)S(1)} %prep.1), channel_id=1, source_target_pairs={{0,12},{1,13},{2,14},{3,15},{4,8},{5,9},{6,10},{7,11},{8,4},{9,5},... | collective-permute-start | bytes 208904 | tf_op jit(solution)/shard_map/ppermute | solution.py:332
  7.4 10.0 %collective-permute-start.3 = (bf16[136,256]{1,0:T(8,128)(2,1)S(1)}, bf16[136,256]{1,0:T(8,128)(2,1)S(1)}, u32[]{:S(2)}, u32[]{:S(2)}) collective-permute-start(bf16[136,256]{1,0:T(8,128)(2,1)S(1)} %prep.1), channel_id=1, source_target_pairs={{0,2},{1,3},{2,0},{3,1},{4,6},{5,7},{6,4},{7,5},{8,10},{9,11},{10,... | collective-permute-start | bytes 208904 | tf_op jit(solution)/shard_map/ppermute | solution.py:332
  9.2 0.7 %copy-start = (s32[16,16]{1,0:T(8,128)S(1)}, s32[16,16]{1,0:T(8,128)}, u32[]{:S(2)}) copy-start(s32[16,16]{1,0:T(8,128)} %bins_ref.1) | copy-start | bytes 3076
  9.9 0.7 %copy-start.1 = (s32[16]{0:T(128)S(1)}, s32[16]{0:T(128)}, u32[]{:S(2)}) copy-start(s32[16]{0:T(128)} %owner_ref.1) | copy-start | bytes 196
  13.6 7.8 %collective-permute-start.7 = (bf16[4,136,256]{2,1,0:T(8,128)(2,1)S(1)}, bf16[4,136,256]{2,1,0:T(8,128)(2,1)S(1)}, u32[]{:S(2)}, u32[]{:S(2)}) collective-permute-start(bf16[4,136,256]{2,1,0:T(8,128)(2,1)S(1)} %pad_maximum_fusion.x_hbm), channel_id=1, source_target_pairs={{0,1},{1,0},{2,3},{3,2},{4,5},{5,4},{6,7},{7,6},{8,9},{9,8},{10,11... | collective-permute-start | bytes 835592 | tf_op jit(solution)/shard_map/ppermute | solution.py:332
  13.7 4.8 %collective-permute-start.4 = (bf16[136,256]{1,0:T(8,128)(2,1)S(1)}, bf16[136,256]{1,0:T(8,128)(2,1)S(1)}, u32[]{:S(2)}, u32[]{:S(2)}) collective-permute-start(bf16[136,256]{1,0:T(8,128)(2,1)S(1)} %collective-permute-done), channel_id=1, source_target_pairs={{0,2},{1,3},{2,0},{3,1},{4,6},{5,7},{6,4},{7,5},{8,10},{9,11},{10,... | collective-permute-start | bytes 208904 | tf_op jit(solution)/shard_map/ppermute | solution.py:332
  15.3 5.1 %collective-permute-start.5 = (bf16[136,256]{1,0:T(8,128)(2,1)S(1)}, bf16[136,256]{1,0:T(8,128)(2,1)S(1)}, u32[]{:S(2)}, u32[]{:S(2)}) collective-permute-start(bf16[136,256]{1,0:T(8,128)(2,1)S(1)} %collective-permute-done.1), channel_id=1, source_target_pairs={{0,2},{1,3},{2,0},{3,1},{4,6},{5,7},{6,4},{7,5},{8,10},{9,11},{10,... | collective-permute-start | bytes 208904 | tf_op jit(solution)/shard_map/ppermute | solution.py:332
  15.8 5.5 %collective-permute-start.6 = (bf16[136,256]{1,0:T(8,128)(2,1)S(1)}, bf16[136,256]{1,0:T(8,128)(2,1)S(1)}, u32[]{:S(2)}, u32[]{:S(2)}) collective-permute-start(bf16[136,256]{1,0:T(8,128)(2,1)S(1)} %collective-permute-done.2), channel_id=1, source_target_pairs={{0,2},{1,3},{2,0},{3,1},{4,6},{5,7},{6,4},{7,5},{8,10},{9,11},{10,... | collective-permute-start | bytes 208904 | tf_op jit(solution)/shard_map/ppermute | solution.py:332
  21.3 1.6 %collective-permute-start.8 = (bf16[4,136,256]{2,1,0:T(8,128)(2,1)S(1)}, bf16[4,136,256]{2,1,0:T(8,128)(2,1)S(1)}, u32[]{:S(2)}, u32[]{:S(2)}) collective-permute-start(bf16[4,136,256]{2,1,0:T(8,128)(2,1)S(1)} %pad_maximum_fusion.1), channel_id=1, source_target_pairs={{0,1},{1,0},{2,3},{3,2},{4,5},{5,4},{6,7},{7,6},{8,9},{9,8},{10,11... | collective-permute-start | bytes 835592 | tf_op jit(solution)/shard_map/ppermute | solution.py:332

commit v3 on v2

--- a/solution.py
+++ b/solution.py
@@ -81,42 +81,40 @@
 
 def pairs_kernel(devices, own_ref, bins_ref, owner_ref, list_ref):
     own = own_ref[0]
-    early_at, late_at = 2, 3 + devices * devices
-    first_late = devices - devices // GROUPS
+    members = devices // GROUPS
     own_bin = jnp.int32(0)
     for i in range(devices):
         own_bin = jnp.where(owner_ref[i] == own, i, own_bin)
 
     def row(i, found):
-        early, late = found
+        found = list(found)
         p = own ^ piece_offset(devices, i)
         for j in range(devices):
+            group = j // members
             q = own ^ piece_offset(devices, jnp.int32(j))
-            hit = jnp.where(bins_ref[p, q] == own_bin, 1, 0)
-            code = i * devices + j
-            if j < first_late:
-                list_ref[early_at + early] = code
-                early = early + hit
-            else:
-                list_ref[late_at + late] = code
-                late = late + hit
-        return early, late
-
-    early, late = lax.fori_loop(0, devices, row, (jnp.int32(0), jnp.int32(0)))
-    list_ref[0] = early
-    list_ref[1] = late
+            list_ref[GROUPS + group * devices * members + found[group]] = i * devices + j
+            found[group] = found[group] + jnp.where(bins_ref[p, q] == own_bin, 1, 0)
+        return tuple(found)
+
+    found = lax.fori_loop(0, devices, row, (jnp.int32(0),) * GROUPS)
+    for group in range(GROUPS):
+        list_ref[group] = found[group]
 
 
 def find_pairs(devices, own, bin_ids, owner_table):
     return pl.pallas_call(
         functools.partial(pairs_kernel, devices),
-        out_shape=jax.ShapeDtypeStruct((2 * devices * devices + 4,), jnp.int32),
+        out_shape=jax.ShapeDtypeStruct((GROUPS + devices * devices + 1,), jnp.int32),
         in_specs=[SMEM] * 3,
         out_specs=SMEM,
         compiler_params=pltpu.CompilerParams(vmem_limit_bytes=1 << 20),
         cost_estimate=pl.CostEstimate(flops=10_000_000, bytes_accessed=1 << 20, transcendentals=0),
         name="pairs",
-    )(own, bin_ids, owner_table)
+    )(
+        own,
+        pltpu.with_memory_space_constraint(bin_ids, pltpu.HBM),
+        pltpu.with_memory_space_constraint(owner_table, pltpu.HBM),
+    )
 
 
 def split(value):
@@ -148,10 +146,7 @@
     return lambda i, start, stop: ref[i, start:stop, :].astype(jnp.float32)
 
 
-def turn_kernel(x_hbm, turned_ref, x_ref, high_ref, low_ref, sem):
-    copy = pltpu.make_async_copy(x_hbm, x_ref, sem)
-    copy.start()
-    copy.wait()
+def turn_kernel(x_ref, turned_ref, high_ref, low_ref):
     turn_group(loader(x_ref), x_ref.shape[0], turned_ref, high_ref, low_ref)
 
 
@@ -160,13 +155,11 @@
     return pl.pallas_call(
         turn_kernel,
         out_shape=jax.ShapeDtypeStruct((2 * LANES, members * ROWS), jnp.bfloat16),
-        in_specs=[ANY],
+        in_specs=[VMEM],
         out_specs=VMEM,
         scratch_shapes=[
-            pltpu.VMEM(pieces.shape, jnp.bfloat16),
             pltpu.VMEM((members * ROWS, LANES), jnp.bfloat16),
             pltpu.VMEM((members * ROWS, LANES), jnp.bfloat16),
-            pltpu.SemaphoreType.DMA,
         ],
         compiler_params=pltpu.CompilerParams(vmem_limit_bytes=(2 << 20) + members * (1 << 19)),
         cost_estimate=pl.CostEstimate(
@@ -176,7 +169,7 @@
     )(pieces)
 
 
-def add_pairs(devices, first, base, count, list_ref, x_ref, sums_ref):
+def add_pairs(devices, first, base, start, stop, list_ref, x_ref, sums_ref):
     def add(place, carry):
         code = list_ref[base + place]
         i, j = lax.div(code, devices), lax.rem(code, devices) - first
@@ -184,75 +177,52 @@
         sums_ref[i] = sums_ref[i] + x_ref[j, 0:ROWS, :].astype(jnp.float32) * scale
         return carry
 
-    lax.fori_loop(0, count, add, 0)
-
-
-def middle_kernel(devices, list_ref, near_hbm, side_hbm, turned_y_ref, turned_s_ref, sums_ref, x_ref, high_ref, low_ref, sem):
-    members = devices // GROUPS
-    copies = [
-        pltpu.make_async_copy(near_hbm, x_ref.at[pl.ds(0, 2 * members)], sem.at[0]),
-        pltpu.make_async_copy(side_hbm, x_ref.at[pl.ds(2 * members, members)], sem.at[1]),
-    ]
-    for copy in copies:
-        copy.start()
+    lax.fori_loop(start, stop, add, 0)
+
+
+def middle_kernel(
+    devices, list_ref, column_ref, plane_ref, side_ref,
+    turned_y_ref, turned_s_ref, sums_ref, high_ref, low_ref,
+):
+    members = devices // GROUPS
     sums_ref[...] = jnp.zeros_like(sums_ref)
-    for copy in copies:
-        copy.wait()
-    for turned_ref, base in ((turned_y_ref, members), (turned_s_ref, 2 * members)):
-        turn_group(
-            lambda i, a, b, base=base: x_ref[base + i, a:b, :].astype(jnp.float32),
-            members,
-            turned_ref,
-            high_ref,
-            low_ref,
-        )
-    add_pairs(devices, 0, 2, list_ref[0], list_ref, x_ref, sums_ref)
-
-
-def middle(devices, pairs, near, side):
+    turn_group(loader(plane_ref), members, turned_y_ref, high_ref, low_ref)
+    turn_group(loader(side_ref), members, turned_s_ref, high_ref, low_ref)
+    for group, ref in enumerate((column_ref, plane_ref, side_ref)):
+        base = GROUPS + group * devices * members
+        add_pairs(devices, group * members, base, 0, list_ref[group], list_ref, ref, sums_ref)
+
+
+def middle(devices, pairs, column, plane, side):
     members = devices // GROUPS
     turned = jax.ShapeDtypeStruct((2 * LANES, members * ROWS), jnp.bfloat16)
     return pl.pallas_call(
         functools.partial(middle_kernel, devices),
         out_shape=(turned, turned, jax.ShapeDtypeStruct((devices, ROWS, LANES), jnp.float32)),
-        in_specs=[SMEM, ANY, ANY],
+        in_specs=[SMEM, VMEM, VMEM, VMEM],
         out_specs=(VMEM, VMEM, VMEM),
         scratch_shapes=[
-            pltpu.VMEM((3 * members, HEAD, LANES), jnp.bfloat16),
             pltpu.VMEM((members * ROWS, LANES), jnp.bfloat16),
             pltpu.VMEM((members * ROWS, LANES), jnp.bfloat16),
-            pltpu.SemaphoreType.DMA((2,)),
         ],
         compiler_params=pltpu.CompilerParams(vmem_limit_bytes=(2 << 20) + devices * (1 << 19)),
         cost_estimate=pl.CostEstimate(
             flops=devices * 2_000_000, bytes_accessed=devices << 18, transcendentals=0
         ),
         name="middle",
-    )(pairs, near, side)
+    )(pairs, column, plane, side)
 
 
 def stack_kernel(
-    devices, span, list_ref, t0_ref, t1_ref, t2_ref, sums_hbm, last_hbm, out_ref,
-    x_ref, sums_ref, a0_ref, a1_ref, a2_ref, a3_ref, high_ref, low_ref, yh_ref, yl_ref, sem,
+    devices, span, list_ref, a0_ref, a1_ref, a2_ref, _, x_ref, out_ref, sums_ref,
+    a3_ref, high_ref, low_ref, yh_ref, yl_ref,
 ):
     members = devices // GROUPS
     depth = members * ROWS
     slab = members * COARSE
-    copies = [
-        pltpu.make_async_copy(last_hbm, x_ref, sem.at[0]),
-        pltpu.make_async_copy(sums_hbm, sums_ref, sem.at[1]),
-        pltpu.make_async_copy(t0_ref, a0_ref, sem.at[2]),
-        pltpu.make_async_copy(t1_ref, a1_ref, sem.at[3]),
-        pltpu.make_async_copy(t2_ref, a2_ref, sem.at[4]),
-    ]
-    for copy in copies:
-        copy.start()
-    copies[0].wait()
-    copies[1].wait()
-    late_at = 3 + devices * devices
-    add_pairs(devices, 3 * members, late_at, list_ref[1], list_ref, x_ref, sums_ref)
-    for copy in copies[2:]:
-        copy.wait()
+    last = GROUPS - 1
+    base = GROUPS + last * devices * members
+    add_pairs(devices, last * members, base, 0, list_ref[last], list_ref, x_ref, sums_ref)
     turn_group(loader(x_ref), members, a3_ref, high_ref, low_ref)
 
     def put(group, member, u1, value):
@@ -289,7 +259,7 @@
     stack = jnp.zeros((CH, OUT_LANES), jnp.float32)
     for v in range(STEP):
         stack = stack + product[CH * v : CH * (v + 1), CH * v : CH * v + OUT_LANES]
-    count = (list_ref[0] + list_ref[1]).astype(jnp.float32)
+    count = sum(list_ref[group] for group in range(GROUPS)).astype(jnp.float32)
     stack = stack / jnp.sqrt(jnp.full((CH, OUT_LANES), count * span, jnp.float32))
     for a in range(CH):
         out_ref[0:1, a * OUT_LANES : (a + 1) * OUT_LANES] = stack[a : a + 1]
@@ -299,28 +269,26 @@
     members = devices // GROUPS
     depth = members * ROWS
     extended = members * COARSE * (FINE + 2 * REACH)
-    left = pltpu.VMEM((2 * LANES, depth), jnp.bfloat16)
-    return pl.pallas_call(
+    stack, _ = pl.pallas_call(
         functools.partial(stack_kernel, devices, float(span)),
-        out_shape=jax.ShapeDtypeStruct((1, CH * OUT_LANES), jnp.float32),
-        in_specs=[SMEM] + [ANY] * 5,
-        out_specs=VMEM,
+        out_shape=(
+            jax.ShapeDtypeStruct((1, CH * OUT_LANES), jnp.float32),
+            jax.ShapeDtypeStruct(sums.shape, jnp.float32),
+        ),
+        in_specs=[SMEM] + [VMEM] * 5,
+        out_specs=(VMEM, VMEM),
+        input_output_aliases={4: 1},
         scratch_shapes=[
-            pltpu.VMEM((members, HEAD, LANES), jnp.bfloat16),
-            pltpu.VMEM((devices, ROWS, LANES), jnp.float32),
-            left,
-            left,
-            left,
-            left,
+            pltpu.VMEM((2 * LANES, depth), jnp.bfloat16),
             pltpu.VMEM((depth, LANES), jnp.bfloat16),
             pltpu.VMEM((depth, LANES), jnp.bfloat16),
             pltpu.VMEM((GROUPS, extended, LANES), jnp.bfloat16),
             pltpu.VMEM((GROUPS, extended, LANES), jnp.bfloat16),
-            pltpu.SemaphoreType.DMA((5,)),
         ],
         compiler_params=pltpu.CompilerParams(vmem_limit_bytes=(8 << 20) + devices * (5 << 17)),
         name="stack",
     )(pairs, *turned, sums, last)
+    return stack
 
 
 def on_device(samples, scales, bin_ids, owner_table):
@@ -334,22 +302,17 @@
     piece = prep(samples, scales)
     pairs = find_pairs(devices, own, bin_ids, owner_table)
     members = devices // GROUPS
-    near = jnp.zeros((2 * members,) + piece.shape, piece.dtype)
-    near = near.at[0].set(piece)
-    column = [piece]
+    own_column = jnp.zeros((members,) + piece.shape, piece.dtype).at[0].set(piece)
     plane = [swap(piece, 2)]
     for i in range(1, members):
         one = swap(piece, 4 * i)
-        column.append(one)
         plane.append(swap(one, 2))
-        near = near.at[i].set(one)
-    for i, one in enumerate(plane):
-        near = near.at[members + i].set(one)
-    own_column = jnp.stack(column)
+        own_column = own_column.at[i].set(one)
     side_column = swap(own_column, 1)
-    side_plane = swap(jnp.stack(plane), 1)
+    own_plane = jnp.stack(plane)
+    side_plane = swap(own_plane, 1)
     turned_0 = turn(own_column)
-    turned_1, turned_2, sums = middle(devices, pairs, near, side_column)
+    turned_1, turned_2, sums = middle(devices, pairs, own_column, own_plane, side_column)
     return stack_bin(
         devices, span, pairs, (turned_0, turned_1, turned_2), sums, side_plane
     )

time: 29.2 us -> 28.7 us (0.983)
  local copies, waits for them, and re-layouts: 1.43 us -> 0.04 us
  waiting for transfers between devices: 4.39 us -> 5.34 us
  Pallas kernels: 11.8 us -> 11.4 us
  starting transfers between devices: 11.2 us -> 11.5 us
    unnamed x4 -> x0, local copies, waits for them, and re-layouts: 1.35 us -> none
    ppermute x9, waiting for transfers between devices: 4.39 us -> 5.34 us  [swap(): lax.ppermute(value, 'chan', [(i, i ^ offset) for i in range(devices)])]
    ppermute x9, starting transfers between devices: 11.2 us -> 11.5 us  [swap(): lax.ppermute(value, 'chan', [(i, i ^ offset) for i in range(devices)])]
  transfers between devices with their start and end apart: 9 -> 9, of which waited for: 5 -> 4; matrix products, arithmetic and copies ran while one was open for 1% -> 0% of each run, Pallas kernels for 14% -> 14%
where the time goes in v3:
time: 28.7 us; the launch traced here: 28.5 us
  starting transfers between devices  11.5 us (40%)
  Pallas kernels  11.4 us (40%)
  waiting for transfers between devices  5.34 us (19%)
    ppermute x9, starting transfers between devices, swap(): lax.ppermute(value, 'chan', [(i, i ^ offset) for i in range(devices)])  11.5 us
    pallas_call x1, Pallas kernels, stack_bin(): pl.pallas_call(functools.partial(stack_kernel, devices, float(span)), out...  5.82 us
    ppermute x9, waiting for transfers between devices, swap(): lax.ppermute(value, 'chan', [(i, i ^ offset) for i in range(devices)])  5.34 us
    pallas_call x1, Pallas kernels, find_pairs(): pl.pallas_call(functools.partial(pairs_kernel, devices), out_shape=jax.Sh...  2.59 us
    pallas_call x1, Pallas kernels, prep(): pl.pallas_call(prep_kernel, out_shape=jax.ShapeDtypeStruct((HEAD, LANES),...  1.66 us
    pallas_call x1, Pallas kernels, middle(): pl.pallas_call(functools.partial(middle_kernel, devices), out_shape=(turn...  1.15 us
  transfers between devices with their start and end apart: 9, of which 4 were waited for; matrix products, arithmetic and copies ran while one was open for 0% of the time, Pallas kernels for 14%

profile of v3, /device:TPU:0, one launch (start us, length us, event | category | flops | bytes accessed | tf_op | source)
XLA Modules:
  0.0 28.5 jit_solution(16584315623789021387)
XLA Ops:
  0.0 1.7 %prep.1 = bf16[136,256]{1,0:T(8,128)(2,1)S(1)} custom-call(bf16[16,2048]{1,0:T(8,128)(2,1)} %samples_ref.1, bf16[1,16]{1,0:T(2,128)(2,1)} %bitcast.18), custom_call_target="tpu_custom_call" | custom-call | tf_op jit(solution)/shard_map/prep/pallas_call | solution.py:63
  1.7 5.1 %collective-permute-start.2 = (bf16[136,256]{1,0:T(8,128)(2,1)S(1)}, bf16[136,256]{1,0:T(8,128)(2,1)S(1)}, u32[]{:S(2)}, u32[]{:S(2)}) collective-permute-start(bf16[136,256]{1,0:T(8,128)(2,1)S(1)} %prep.1), channel_id=1, source_target_pairs={{0,12},{1,13},{2,14},{3,15},{4,8},{5,9},{6,10},{7,11},{8,4},{9,5},... | collective-permute-start | bytes 208904 | tf_op jit(solution)/shard_map/ppermute | solution.py:300
  6.8 0.0 collective-permute-start.1
  6.8 0.6 %collective-permute-start = (bf16[136,256]{1,0:T(8,128)(2,1)S(1)}, bf16[136,256]{1,0:T(8,128)(2,1)S(1)}, u32[]{:S(2)}, u32[]{:S(2)}) collective-permute-start(bf16[136,256]{1,0:T(8,128)(2,1)S(1)} %prep.1), channel_id=1, source_target_pairs={{0,4},{1,5},{2,6},{3,7},{4,0},{5,1},{6,2},{7,3},{8,12},{9,13},{10,... | collective-permute-start | bytes 208904 | tf_op jit(solution)/shard_map/ppermute | solution.py:300
  7.5 1.7 %collective-permute-start.3 = (bf16[136,256]{1,0:T(8,128)(2,1)S(1)}, bf16[136,256]{1,0:T(8,128)(2,1)S(1)}, u32[]{:S(2)}, u32[]{:S(2)}) collective-permute-start(bf16[136,256]{1,0:T(8,128)(2,1)S(1)} %prep.1), channel_id=1, source_target_pairs={{0,2},{1,3},{2,0},{3,1},{4,6},{5,7},{6,4},{7,5},{8,10},{9,11},{10,... | collective-permute-start | bytes 208904 | tf_op jit(solution)/shard_map/ppermute | solution.py:300
  9.1 0.2 collective-permute-done.2
  9.4 1.9 %collective-permute-start.6 = (bf16[136,256]{1,0:T(8,128)(2,1)S(1)}, bf16[136,256]{1,0:T(8,128)(2,1)S(1)}, u32[]{:S(2)}, u32[]{:S(2)}) collective-permute-start(bf16[136,256]{1,0:T(8,128)(2,1)S(1)} %collective-permute-done.2), channel_id=1, source_target_pairs={{0,2},{1,3},{2,0},{3,1},{4,6},{5,7},{6,4},{7,5},{8,10},{9,11},{10,... | collective-permute-start | bytes 208904 | tf_op jit(solution)/shard_map/ppermute | solution.py:300
  11.3 1.4 %collective-permute-done.1 = bf16[136,256]{1,0:T(8,128)(2,1)S(1)} collective-permute-done((bf16[136,256]{1,0:T(8,128)(2,1)S(1)}, bf16[136,256]{1,0:T(8,128)(2,1)S(1)}, u32[]{:S(2)}, u32[]{:S(2)}) %collective-permute-start.1) | collective-permute-done | bytes 69664 | tf_op jit(solution)/shard_map/ppermute | solution.py:300
  12.7 1.5 %collective-permute-start.5 = (bf16[136,256]{1,0:T(8,128)(2,1)S(1)}, bf16[136,256]{1,0:T(8,128)(2,1)S(1)}, u32[]{:S(2)}, u32[]{:S(2)}) collective-permute-start(bf16[136,256]{1,0:T(8,128)(2,1)S(1)} %collective-permute-done.1), channel_id=1, source_target_pairs={{0,2},{1,3},{2,0},{3,1},{4,6},{5,7},{6,4},{7,5},{8,10},{9,11},{10,... | collective-permute-start | bytes 208904 | tf_op jit(solution)/shard_map/ppermute | solution.py:300
  14.2 0.0 collective-permute-done
  14.2 0.5 %collective-permute-start.4 = (bf16[136,256]{1,0:T(8,128)(2,1)S(1)}, bf16[136,256]{1,0:T(8,128)(2,1)S(1)}, u32[]{:S(2)}, u32[]{:S(2)}) collective-permute-start(bf16[136,256]{1,0:T(8,128)(2,1)S(1)} %collective-permute-done), channel_id=1, source_target_pairs={{0,2},{1,3},{2,0},{3,1},{4,6},{5,7},{6,4},{7,5},{8,10},{9,11},{10,... | collective-permute-start | bytes 208904 | tf_op jit(solution)/shard_map/ppermute | solution.py:300
  14.8 0.1 collective-permute-start.7
  14.9 0.0 collective-permute-done.3
  14.9 0.0 collective-permute-done.6
  14.9 2.9 %collective-permute-done.5 = bf16[136,256]{1,0:T(8,128)(2,1)S(1)} collective-permute-done((bf16[136,256]{1,0:T(8,128)(2,1)S(1)}, bf16[136,256]{1,0:T(8,128)(2,1)S(1)}, u32[]{:S(2)}, u32[]{:S(2)}) %collective-permute-start.5) | collective-permute-done | bytes 69664 | tf_op jit(solution)/shard_map/ppermute | solution.py:300
  17.7 0.8 %collective-permute-done.4 = bf16[136,256]{1,0:T(8,128)(2,1)S(1)} collective-permute-done((bf16[136,256]{1,0:T(8,128)(2,1)S(1)}, bf16[136,256]{1,0:T(8,128)(2,1)S(1)}, u32[]{:S(2)}, u32[]{:S(2)}) %collective-permute-start.4) | collective-permute-done | bytes 69664 | tf_op jit(solution)/shard_map/ppermute | solution.py:300
  18.6 0.1 collective-permute-start.8
  18.7 2.6 %pairs.1.list_ref = s32[261]{0:T(512)S(1)} custom-call(s32[1]{0:T(128)} %bitcast.own_ref, s32[16,16]{1,0:T(8,128)} %bins_ref.1, s32[16]{0:T(128)} %owner_ref.1), custom_call_target="tpu_custom_call" | custom-call | flops 10000000 | bytes 1048576 | tf_op jit(solution)/shard_map/pairs/pallas_call | solution.py:105
  21.3 0.2 turn.1.a0_ref
  21.5 0.0 collective-permute-done.7.side_ref
  21.5 1.1 %middle.1 = (bf16[512,512]{1,0:T(8,128)(2,1)S(1)}, bf16[512,512]{1,0:T(8,128)(2,1)S(1)}, f32[16,128,256]{2,1,0:T(8,128)S(1)}) custom-call(s32[261]{0:T(512)S(1)} %pairs.1.list_ref, bf16[4,136,256]{2,1,0:T(8,128)(2,1)S(1)} %bitcast_dynamic-update-slice_fusion.x_ref.column_ref, bf16[4,136,256]{2,1,0:T(8,128)(2,1)S(1)} %pad_maximum_fusion.plane_ref, ...), custom_call_target="tpu_custom_call" | custom-call | flops 32000000 | bytes 4194304 | tf_op jit(solution)/shard_map/middle/pallas_call | solution.py:199
  22.6 0.0 collective-permute-done.8.x_ref
  22.6 5.8 %stack.21 = (f32[1,16640]{1,0:T(1,128)}, f32[16,128,256]{2,1,0:T(8,128)S(1)}) custom-call(s32[261]{0:T(512)S(1)} %pairs.1.list_ref, bf16[512,512]{1,0:T(8,128)(2,1)S(1)} %turn.1.a0_ref, bf16[512,512]{1,0:T(8,128)(2,1)S(1)} %get-tuple-element.57.a1_ref, bf16[512,512]{1,0:T(8,128)(2,1)S(1)} %get-tuple-element.58.a2_ref, ...), custom_call_target="tpu_custom_call", output_to_operand_aliasing={{1}: (4, {})} | custom-call | tf_op jit(solution)/shard_map/stack/pallas_call | solution.py:272
  (5 shorter events, 0.1 us)
Async XLA Ops:
  1.7 7.7 %collective-permute-start.2 = (bf16[136,256]{1,0:T(8,128)(2,1)S(1)}, bf16[136,256]{1,0:T(8,128)(2,1)S(1)}, u32[]{:S(2)}, u32[]{:S(2)}) collective-permute-start(bf16[136,256]{1,0:T(8,128)(2,1)S(1)} %prep.1), channel_id=1, source_target_pairs={{0,12},{1,13},{2,14},{3,15},{4,8},{5,9},{6,10},{7,11},{8,4},{9,5},... | collective-permute-start | bytes 208904 | tf_op jit(solution)/shard_map/ppermute | solution.py:300
  6.8 5.9 %collective-permute-start.1 = (bf16[136,256]{1,0:T(8,128)(2,1)S(1)}, bf16[136,256]{1,0:T(8,128)(2,1)S(1)}, u32[]{:S(2)}, u32[]{:S(2)}) collective-permute-start(bf16[136,256]{1,0:T(8,128)(2,1)S(1)} %prep.1), channel_id=1, source_target_pairs={{0,8},{1,9},{2,10},{3,11},{4,12},{5,13},{6,14},{7,15},{8,0},{9,1},... | collective-permute-start | bytes 208904 | tf_op jit(solution)/shard_map/ppermute | solution.py:300
  6.8 7.4 %collective-permute-start = (bf16[136,256]{1,0:T(8,128)(2,1)S(1)}, bf16[136,256]{1,0:T(8,128)(2,1)S(1)}, u32[]{:S(2)}, u32[]{:S(2)}) collective-permute-start(bf16[136,256]{1,0:T(8,128)(2,1)S(1)} %prep.1), channel_id=1, source_target_pairs={{0,4},{1,5},{2,6},{3,7},{4,0},{5,1},{6,2},{7,3},{8,12},{9,13},{10,... | collective-permute-start | bytes 208904 | tf_op jit(solution)/shard_map/ppermute | solution.py:300
  7.5 7.4 %collective-permute-start.3 = (bf16[136,256]{1,0:T(8,128)(2,1)S(1)}, bf16[136,256]{1,0:T(8,128)(2,1)S(1)}, u32[]{:S(2)}, u32[]{:S(2)}) collective-permute-start(bf16[136,256]{1,0:T(8,128)(2,1)S(1)} %prep.1), channel_id=1, source_target_pairs={{0,2},{1,3},{2,0},{3,1},{4,6},{5,7},{6,4},{7,5},{8,10},{9,11},{10,... | collective-permute-start | bytes 208904 | tf_op jit(solution)/shard_map/ppermute | solution.py:300
  9.4 5.5 %collective-permute-start.6 = (bf16[136,256]{1,0:T(8,128)(2,1)S(1)}, bf16[136,256]{1,0:T(8,128)(2,1)S(1)}, u32[]{:S(2)}, u32[]{:S(2)}) collective-permute-start(bf16[136,256]{1,0:T(8,128)(2,1)S(1)} %collective-permute-done.2), channel_id=1, source_target_pairs={{0,2},{1,3},{2,0},{3,1},{4,6},{5,7},{6,4},{7,5},{8,10},{9,11},{10,... | collective-permute-start | bytes 208904 | tf_op jit(solution)/shard_map/ppermute | solution.py:300
  12.7 5.0 %collective-permute-start.5 = (bf16[136,256]{1,0:T(8,128)(2,1)S(1)}, bf16[136,256]{1,0:T(8,128)(2,1)S(1)}, u32[]{:S(2)}, u32[]{:S(2)}) collective-permute-start(bf16[136,256]{1,0:T(8,128)(2,1)S(1)} %collective-permute-done.1), channel_id=1, source_target_pairs={{0,2},{1,3},{2,0},{3,1},{4,6},{5,7},{6,4},{7,5},{8,10},{9,11},{10,... | collective-permute-start | bytes 208904 | tf_op jit(solution)/shard_map/ppermute | solution.py:300
  14.2 4.3 %collective-permute-start.4 = (bf16[136,256]{1,0:T(8,128)(2,1)S(1)}, bf16[136,256]{1,0:T(8,128)(2,1)S(1)}, u32[]{:S(2)}, u32[]{:S(2)}) collective-permute-start(bf16[136,256]{1,0:T(8,128)(2,1)S(1)} %collective-permute-done), channel_id=1, source_target_pairs={{0,2},{1,3},{2,0},{3,1},{4,6},{5,7},{6,4},{7,5},{8,10},{9,11},{10,... | collective-permute-start | bytes 208904 | tf_op jit(solution)/shard_map/ppermute | solution.py:300
  14.8 6.7 %collective-permute-start.7 = (bf16[4,136,256]{2,1,0:T(8,128)(2,1)S(1)}, bf16[4,136,256]{2,1,0:T(8,128)(2,1)S(1)}, u32[]{:S(2)}, u32[]{:S(2)}) collective-permute-start(bf16[4,136,256]{2,1,0:T(8,128)(2,1)S(1)} %bitcast_dynamic-update-slice_fusion.x_ref.column_ref), channel_id=1, source_target_pairs={{0,1},{1,0},{2,3},{3,2},{4,5},{5,4},{6,7},{7,6},{8,9},{9,8},{10,11... | collective-permute-start | bytes 835592 | tf_op jit(solution)/shard_map/ppermute | solution.py:300
  18.6 4.0 %collective-permute-start.8 = (bf16[4,136,256]{2,1,0:T(8,128)(2,1)S(1)}, bf16[4,136,256]{2,1,0:T(8,128)(2,1)S(1)}, u32[]{:S(2)}, u32[]{:S(2)}) collective-permute-start(bf16[4,136,256]{2,1,0:T(8,128)(2,1)S(1)} %pad_maximum_fusion.plane_ref), channel_id=1, source_target_pairs={{0,1},{1,0},{2,3},{3,2},{4,5},{5,4},{6,7},{7,6},{8,9},{9,8},{10,11... | collective-permute-start | bytes 835592 | tf_op jit(solution)/shard_map/ppermute | solution.py:300

commit v4 on v3

--- a/solution.py
+++ b/solution.py
@@ -19,6 +19,7 @@
 REACH = LAG // STEP
 SHIFTS = 2 * REACH + 1
 OUT_LANES = LAGS * CH
+BLEND = 32.0
 GROUPS = 4
 
 VMEM = pl.BlockSpec(memory_space=pltpu.VMEM)
@@ -117,9 +118,16 @@
     )
 
 
-def split(value):
+def split_left(value):
     high = value.astype(jnp.bfloat16)
-    return high, (value - high.astype(jnp.float32)).astype(jnp.bfloat16)
+    wide = high.astype(jnp.float32)
+    return high, (wide + BLEND * (value - wide)).astype(jnp.bfloat16)
+
+
+def split_right(value):
+    high = value.astype(jnp.bfloat16)
+    wide = high.astype(jnp.float32)
+    return high, (wide * (1.0 / BLEND) + (value - wide)).astype(jnp.bfloat16)
 
 
 def inside_rows():
@@ -132,7 +140,7 @@
     inside = inside_rows()
     for i in range(members):
         scale = load(i, ROWS, ROWS + 1)
-        high, low = split(jnp.where(inside, load(i, 0, ROWS) * scale, 0.0))
+        high, low = split_left(jnp.where(inside, load(i, 0, ROWS) * scale, 0.0))
         for u1 in range(FINE):
             at = (u1 * members + i) * COARSE
             high_ref[at : at + COARSE, :] = high[u1 * COARSE : (u1 + 1) * COARSE]
@@ -180,27 +188,32 @@
     lax.fori_loop(start, stop, add, 0)
 
 
-def middle_kernel(
-    devices, list_ref, column_ref, plane_ref, side_ref,
-    turned_y_ref, turned_s_ref, sums_ref, high_ref, low_ref,
-):
+def early_kernel(devices, list_ref, column_ref, side_ref, turned_ref, sums_ref, high_ref, low_ref):
     members = devices // GROUPS
     sums_ref[...] = jnp.zeros_like(sums_ref)
-    turn_group(loader(plane_ref), members, turned_y_ref, high_ref, low_ref)
-    turn_group(loader(side_ref), members, turned_s_ref, high_ref, low_ref)
-    for group, ref in enumerate((column_ref, plane_ref, side_ref)):
+    turn_group(loader(side_ref), members, turned_ref, high_ref, low_ref)
+    for group, ref in ((0, column_ref), (2, side_ref)):
         base = GROUPS + group * devices * members
         add_pairs(devices, group * members, base, 0, list_ref[group], list_ref, ref, sums_ref)
 
 
-def middle(devices, pairs, column, plane, side):
-    members = devices // GROUPS
-    turned = jax.ShapeDtypeStruct((2 * LANES, members * ROWS), jnp.bfloat16)
-    return pl.pallas_call(
-        functools.partial(middle_kernel, devices),
-        out_shape=(turned, turned, jax.ShapeDtypeStruct((devices, ROWS, LANES), jnp.float32)),
-        in_specs=[SMEM, VMEM, VMEM, VMEM],
-        out_specs=(VMEM, VMEM, VMEM),
+def plane_kernel(devices, list_ref, plane_ref, _, turned_ref, sums_ref, high_ref, low_ref):
+    members = devices // GROUPS
+    turn_group(loader(plane_ref), members, turned_ref, high_ref, low_ref)
+    base = GROUPS + devices * members
+    add_pairs(devices, members, base, 0, list_ref[1], list_ref, plane_ref, sums_ref)
+
+
+def early(devices, pairs, column, side):
+    members = devices // GROUPS
+    return pl.pallas_call(
+        functools.partial(early_kernel, devices),
+        out_shape=(
+            jax.ShapeDtypeStruct((2 * LANES, members * ROWS), jnp.bfloat16),
+            jax.ShapeDtypeStruct((devices, ROWS, LANES), jnp.float32),
+        ),
+        in_specs=[SMEM, VMEM, VMEM],
+        out_specs=(VMEM, VMEM),
         scratch_shapes=[
             pltpu.VMEM((members * ROWS, LANES), jnp.bfloat16),
             pltpu.VMEM((members * ROWS, LANES), jnp.bfloat16),
@@ -209,8 +222,31 @@
         cost_estimate=pl.CostEstimate(
             flops=devices * 2_000_000, bytes_accessed=devices << 18, transcendentals=0
         ),
-        name="middle",
-    )(pairs, column, plane, side)
+        name="early",
+    )(pairs, column, side)
+
+
+def add_plane(devices, pairs, plane, sums):
+    members = devices // GROUPS
+    return pl.pallas_call(
+        functools.partial(plane_kernel, devices),
+        out_shape=(
+            jax.ShapeDtypeStruct((2 * LANES, members * ROWS), jnp.bfloat16),
+            jax.ShapeDtypeStruct(sums.shape, jnp.float32),
+        ),
+        in_specs=[SMEM, VMEM, VMEM],
+        out_specs=(VMEM, VMEM),
+        input_output_aliases={2: 1},
+        scratch_shapes=[
+            pltpu.VMEM((members * ROWS, LANES), jnp.bfloat16),
+            pltpu.VMEM((members * ROWS, LANES), jnp.bfloat16),
+        ],
+        compiler_params=pltpu.CompilerParams(vmem_limit_bytes=(2 << 20) + devices * (1 << 19)),
+        cost_estimate=pl.CostEstimate(
+            flops=devices * 1_000_000, bytes_accessed=devices << 17, transcendentals=0
+        ),
+        name="plane",
+    )(pairs, plane, sums)
 
 
 def stack_kernel(
@@ -226,7 +262,7 @@
     turn_group(loader(x_ref), members, a3_ref, high_ref, low_ref)
 
     def put(group, member, u1, value):
-        high, low = split(value)
+        high, low = split_right(value)
         at = ((u1 + REACH) * members + member) * COARSE
         yh_ref[group, at : at + COARSE, :] = high
         yl_ref[group, at : at + COARSE, :] = low
@@ -243,17 +279,16 @@
             for u1 in range(FINE - REACH, FINE):
                 put(group, member, u1 - FINE, pltpu.roll(parts[u1], 1, 0))
         for j in range(SHIFTS):
-            both = jnp.dot(
-                turned_ref[...],
-                yh_ref[group, j * slab : j * slab + depth, :],
+            rows = slice(j * slab, j * slab + depth)
+            main = jnp.dot(
+                turned_ref[0:LANES, :], yh_ref[group, rows, :], preferred_element_type=jnp.float32
+            )
+            rest = jnp.dot(
+                turned_ref[LANES : 2 * LANES, :],
+                yl_ref[group, rows, :],
                 preferred_element_type=jnp.float32,
             )
-            rest = jnp.dot(
-                turned_ref[0:LANES, :],
-                yl_ref[group, j * slab : j * slab + depth, :],
-                preferred_element_type=jnp.float32,
-            )
-            part = both[0:LANES] + both[LANES : 2 * LANES] + rest
+            part = main * (1.0 - 1.0 / BLEND) + rest
             products[j] = part if group == 0 else products[j] + part
     product = jnp.concatenate(products, axis=1)
     stack = jnp.zeros((CH, OUT_LANES), jnp.float32)
@@ -312,7 +347,8 @@
     own_plane = jnp.stack(plane)
     side_plane = swap(own_plane, 1)
     turned_0 = turn(own_column)
-    turned_1, turned_2, sums = middle(devices, pairs, own_column, own_plane, side_column)
+    turned_2, sums = early(devices, pairs, own_column, side_column)
+    turned_1, sums = add_plane(devices, pairs, own_plane, sums)
     return stack_bin(
         devices, span, pairs, (turned_0, turned_1, turned_2), sums, side_plane
     )

time: 28.7 us -> 27.8 us (0.969)
  starting transfers between devices: 11.5 us -> 10.7 us
  waiting for transfers between devices: 5.34 us -> 5.89 us
  Pallas kernels: 11.4 us -> 10.9 us
    pallas_call x1, Pallas kernels: 5.82 us -> 4.55 us  [stack_bin(): pl.pallas_call(functools.partial(stack_kernel, devices, float(span)), out...]
    ppermute x9, starting transfers between devices: 11.5 us -> 10.7 us  [swap(): lax.ppermute(value, 'chan', [(i, i ^ offset) for i in range(devices)])]
    pallas_call x1 -> x2, Pallas kernels: 1.15 us -> 1.87 us  [the longest x1 1.04 us: early(): pl.pallas_call(functools.partial(early_kernel, devices), out_shape=(jax.S...]
    ppermute x9, waiting for transfers between devices: 5.34 us -> 5.89 us  [swap(): lax.ppermute(value, 'chan', [(i, i ^ offset) for i in range(devices)])]
  transfers between devices with their start and end apart: 9 -> 9, of which waited for: 4 -> 3; matrix products, arithmetic and copies ran while one was open for 0% -> 0% of each run, Pallas kernels for 14% -> 17%
where the time goes in v4:
time: 27.8 us; the launch traced here: 27.6 us
  Pallas kernels  10.9 us (39%)
  starting transfers between devices  10.7 us (38%)
  waiting for transfers between devices  5.89 us (21%)
    ppermute x9, starting transfers between devices, swap(): lax.ppermute(value, 'chan', [(i, i ^ offset) for i in range(devices)])  10.7 us
    ppermute x9, waiting for transfers between devices, swap(): lax.ppermute(value, 'chan', [(i, i ^ offset) for i in range(devices)])  5.89 us
    pallas_call x1, Pallas kernels, stack_bin(): pl.pallas_call(functools.partial(stack_kernel, devices, float(span)), out...  4.55 us
    pallas_call x1, Pallas kernels, find_pairs(): pl.pallas_call(functools.partial(pairs_kernel, devices), out_shape=jax.Sh...  2.59 us
    pallas_call x1, Pallas kernels, prep(): pl.pallas_call(prep_kernel, out_shape=jax.ShapeDtypeStruct((HEAD, LANES),...  1.66 us
    pallas_call x1, Pallas kernels, early(): pl.pallas_call(functools.partial(early_kernel, devices), out_shape=(jax.S...  1.04 us
    pallas_call x1, Pallas kernels, add_plane(): pl.pallas_call(functools.partial(plane_kernel, devices), out_shape=(jax.S...  0.83 us
  transfers between devices with their start and end apart: 9, of which 3 were waited for; matrix products, arithmetic and copies ran while one was open for 0% of the time, Pallas kernels for 17%

profile of v4, /device:TPU:0, one launch (start us, length us, event | category | flops | bytes accessed | tf_op | source)
XLA Modules:
  0.0 27.6 jit_solution(15241801675459407546)
XLA Ops:
  0.0 1.7 %prep.1 = bf16[136,256]{1,0:T(8,128)(2,1)S(1)} custom-call(bf16[16,2048]{1,0:T(8,128)(2,1)} %samples_ref.1, bf16[1,16]{1,0:T(2,128)(2,1)} %bitcast.18), custom_call_target="tpu_custom_call" | custom-call | tf_op jit(solution)/shard_map/prep/pallas_call | solution.py:64
  1.7 3.1 %collective-permute-start = (bf16[136,256]{1,0:T(8,128)(2,1)S(1)}, bf16[136,256]{1,0:T(8,128)(2,1)S(1)}, u32[]{:S(2)}, u32[]{:S(2)}) collective-permute-start(bf16[136,256]{1,0:T(8,128)(2,1)S(1)} %prep.1), channel_id=1, source_target_pairs={{0,4},{1,5},{2,6},{3,7},{4,0},{5,1},{6,2},{7,3},{8,12},{9,13},{10,... | collective-permute-start | bytes 208904 | tf_op jit(solution)/shard_map/ppermute | solution.py:335
  4.8 2.6 %collective-permute-start.1 = (bf16[136,256]{1,0:T(8,128)(2,1)S(1)}, bf16[136,256]{1,0:T(8,128)(2,1)S(1)}, u32[]{:S(2)}, u32[]{:S(2)}) collective-permute-start(bf16[136,256]{1,0:T(8,128)(2,1)S(1)} %prep.1), channel_id=1, source_target_pairs={{0,8},{1,9},{2,10},{3,11},{4,12},{5,13},{6,14},{7,15},{8,0},{9,1},... | collective-permute-start | bytes 208904 | tf_op jit(solution)/shard_map/ppermute | solution.py:335
  7.4 0.0 collective-permute-start.2
  7.4 1.7 %collective-permute-start.3 = (bf16[136,256]{1,0:T(8,128)(2,1)S(1)}, bf16[136,256]{1,0:T(8,128)(2,1)S(1)}, u32[]{:S(2)}, u32[]{:S(2)}) collective-permute-start(bf16[136,256]{1,0:T(8,128)(2,1)S(1)} %prep.1), channel_id=1, source_target_pairs={{0,2},{1,3},{2,0},{3,1},{4,6},{5,7},{6,4},{7,5},{8,10},{9,11},{10,... | collective-permute-start | bytes 208904 | tf_op jit(solution)/shard_map/ppermute | solution.py:335
  9.1 0.0 collective-permute-done
  9.1 0.4 %collective-permute-start.4 = (bf16[136,256]{1,0:T(8,128)(2,1)S(1)}, bf16[136,256]{1,0:T(8,128)(2,1)S(1)}, u32[]{:S(2)}, u32[]{:S(2)}) collective-permute-start(bf16[136,256]{1,0:T(8,128)(2,1)S(1)} %collective-permute-done), channel_id=1, source_target_pairs={{0,2},{1,3},{2,0},{3,1},{4,6},{5,7},{6,4},{7,5},{8,10},{9,11},{10,... | collective-permute-start | bytes 208904 | tf_op jit(solution)/shard_map/ppermute | solution.py:335
  9.5 2.8 %collective-permute-done.1 = bf16[136,256]{1,0:T(8,128)(2,1)S(1)} collective-permute-done((bf16[136,256]{1,0:T(8,128)(2,1)S(1)}, bf16[136,256]{1,0:T(8,128)(2,1)S(1)}, u32[]{:S(2)}, u32[]{:S(2)}) %collective-permute-start.1) | collective-permute-done | bytes 69664 | tf_op jit(solution)/shard_map/ppermute | solution.py:335
  12.3 1.5 %collective-permute-start.5 = (bf16[136,256]{1,0:T(8,128)(2,1)S(1)}, bf16[136,256]{1,0:T(8,128)(2,1)S(1)}, u32[]{:S(2)}, u32[]{:S(2)}) collective-permute-start(bf16[136,256]{1,0:T(8,128)(2,1)S(1)} %collective-permute-done.1), channel_id=1, source_target_pairs={{0,2},{1,3},{2,0},{3,1},{4,6},{5,7},{6,4},{7,5},{8,10},{9,11},{10,... | collective-permute-start | bytes 208904 | tf_op jit(solution)/shard_map/ppermute | solution.py:335
  13.8 0.0 collective-permute-done.2
  13.8 1.3 %collective-permute-start.6 = (bf16[136,256]{1,0:T(8,128)(2,1)S(1)}, bf16[136,256]{1,0:T(8,128)(2,1)S(1)}, u32[]{:S(2)}, u32[]{:S(2)}) collective-permute-start(bf16[136,256]{1,0:T(8,128)(2,1)S(1)} %collective-permute-done.2), channel_id=1, source_target_pairs={{0,2},{1,3},{2,0},{3,1},{4,6},{5,7},{6,4},{7,5},{8,10},{9,11},{10,... | collective-permute-start | bytes 208904 | tf_op jit(solution)/shard_map/ppermute | solution.py:335
  15.1 0.0 collective-permute-start.7
  15.1 0.0 collective-permute-done.3
  15.1 0.0 collective-permute-done.4
  15.1 1.5 %collective-permute-done.5 = bf16[136,256]{1,0:T(8,128)(2,1)S(1)} collective-permute-done((bf16[136,256]{1,0:T(8,128)(2,1)S(1)}, bf16[136,256]{1,0:T(8,128)(2,1)S(1)}, u32[]{:S(2)}, u32[]{:S(2)}) %collective-permute-start.5) | collective-permute-done | bytes 69664 | tf_op jit(solution)/shard_map/ppermute | solution.py:335
  16.6 1.6 %collective-permute-done.6 = bf16[136,256]{1,0:T(8,128)(2,1)S(1)} collective-permute-done((bf16[136,256]{1,0:T(8,128)(2,1)S(1)}, bf16[136,256]{1,0:T(8,128)(2,1)S(1)}, u32[]{:S(2)}, u32[]{:S(2)}) %collective-permute-start.6) | collective-permute-done | bytes 69664 | tf_op jit(solution)/shard_map/ppermute | solution.py:335
  18.3 0.1 collective-permute-start.8
  18.3 2.6 %pairs.1.list_ref = s32[261]{0:T(512)S(1)} custom-call(s32[1]{0:T(128)} %bitcast.own_ref, s32[16,16]{1,0:T(8,128)} %bins_ref.1, s32[16]{0:T(128)} %owner_ref.1), custom_call_target="tpu_custom_call" | custom-call | flops 10000000 | bytes 1048576 | tf_op jit(solution)/shard_map/pairs/pallas_call | solution.py:106
  20.9 0.3 turn.1.a0_ref
  21.2 0.0 collective-permute-done.7.side_ref
  21.2 1.0 %early.1 = (bf16[512,512]{1,0:T(8,128)(2,1)S(1)}, f32[16,128,256]{2,1,0:T(8,128)S(1)}) custom-call(s32[261]{0:T(512)S(1)} %pairs.1.list_ref, bf16[4,136,256]{2,1,0:T(8,128)(2,1)S(1)} %bitcast_dynamic-update-slice_fusion.x_ref.column_ref, bf16[4,136,256]{2,1,0:T(8,128)(2,1)S(1)} %collective-permute-done.7.side_ref), custom_call_target="tpu_custom_call" | custom-call | flops 32000000 | bytes 4194304 | tf_op jit(solution)/shard_map/early/pallas_call | solution.py:209
  22.2 0.8 %plane.1 = (bf16[512,512]{1,0:T(8,128)(2,1)S(1)}, f32[16,128,256]{2,1,0:T(8,128)S(1)}) custom-call(s32[261]{0:T(512)S(1)} %pairs.1.list_ref, bf16[4,136,256]{2,1,0:T(8,128)(2,1)S(1)} %pad_maximum_fusion.plane_ref, f32[16,128,256]{2,1,0:T(8,128)S(1)} %get-tuple-element.58._), custom_call_target="tpu_custom_call", output_to_operand_aliasing={{1}: (2, {})} | custom-call | flops 16000000 | bytes 2097152 | tf_op jit(solution)/shard_map/plane/pallas_call | solution.py:231
  23.1 0.0 collective-permute-done.8.x_ref
  23.1 4.5 %stack.21 = (f32[1,16640]{1,0:T(1,128)}, f32[16,128,256]{2,1,0:T(8,128)S(1)}) custom-call(s32[261]{0:T(512)S(1)} %pairs.1.list_ref, bf16[512,512]{1,0:T(8,128)(2,1)S(1)} %turn.1.a0_ref, bf16[512,512]{1,0:T(8,128)(2,1)S(1)} %get-tuple-element.59.a1_ref, bf16[512,512]{1,0:T(8,128)(2,1)S(1)} %get-tuple-element.60.a2_ref, ...), custom_call_target="tpu_custom_call", output_to_operand_aliasing={{1}: (4, {})} | custom-call | tf_op jit(solution)/shard_map/stack/pallas_call | solution.py:307
  (5 shorter events, 0.1 us)
Async XLA Ops:
  1.7 7.5 %collective-permute-start = (bf16[136,256]{1,0:T(8,128)(2,1)S(1)}, bf16[136,256]{1,0:T(8,128)(2,1)S(1)}, u32[]{:S(2)}, u32[]{:S(2)}) collective-permute-start(bf16[136,256]{1,0:T(8,128)(2,1)S(1)} %prep.1), channel_id=1, source_target_pairs={{0,4},{1,5},{2,6},{3,7},{4,0},{5,1},{6,2},{7,3},{8,12},{9,13},{10,... | collective-permute-start | bytes 208904 | tf_op jit(solution)/shard_map/ppermute | solution.py:335
  4.8 7.5 %collective-permute-start.1 = (bf16[136,256]{1,0:T(8,128)(2,1)S(1)}, bf16[136,256]{1,0:T(8,128)(2,1)S(1)}, u32[]{:S(2)}, u32[]{:S(2)}) collective-permute-start(bf16[136,256]{1,0:T(8,128)(2,1)S(1)} %prep.1), channel_id=1, source_target_pairs={{0,8},{1,9},{2,10},{3,11},{4,12},{5,13},{6,14},{7,15},{8,0},{9,1},... | collective-permute-start | bytes 208904 | tf_op jit(solution)/shard_map/ppermute | solution.py:335
  7.4 6.5 %collective-permute-start.2 = (bf16[136,256]{1,0:T(8,128)(2,1)S(1)}, bf16[136,256]{1,0:T(8,128)(2,1)S(1)}, u32[]{:S(2)}, u32[]{:S(2)}) collective-permute-start(bf16[136,256]{1,0:T(8,128)(2,1)S(1)} %prep.1), channel_id=1, source_target_pairs={{0,12},{1,13},{2,14},{3,15},{4,8},{5,9},{6,10},{7,11},{8,4},{9,5},... | collective-permute-start | bytes 208904 | tf_op jit(solution)/shard_map/ppermute | solution.py:335
  7.4 7.7 %collective-permute-start.3 = (bf16[136,256]{1,0:T(8,128)(2,1)S(1)}, bf16[136,256]{1,0:T(8,128)(2,1)S(1)}, u32[]{:S(2)}, u32[]{:S(2)}) collective-permute-start(bf16[136,256]{1,0:T(8,128)(2,1)S(1)} %prep.1), channel_id=1, source_target_pairs={{0,2},{1,3},{2,0},{3,1},{4,6},{5,7},{6,4},{7,5},{8,10},{9,11},{10,... | collective-permute-start | bytes 208904 | tf_op jit(solution)/shard_map/ppermute | solution.py:335
  9.1 6.0 %collective-permute-start.4 = (bf16[136,256]{1,0:T(8,128)(2,1)S(1)}, bf16[136,256]{1,0:T(8,128)(2,1)S(1)}, u32[]{:S(2)}, u32[]{:S(2)}) collective-permute-start(bf16[136,256]{1,0:T(8,128)(2,1)S(1)} %collective-permute-done), channel_id=1, source_target_pairs={{0,2},{1,3},{2,0},{3,1},{4,6},{5,7},{6,4},{7,5},{8,10},{9,11},{10,... | collective-permute-start | bytes 208904 | tf_op jit(solution)/shard_map/ppermute | solution.py:335
  12.3 4.3 %collective-permute-start.5 = (bf16[136,256]{1,0:T(8,128)(2,1)S(1)}, bf16[136,256]{1,0:T(8,128)(2,1)S(1)}, u32[]{:S(2)}, u32[]{:S(2)}) collective-permute-start(bf16[136,256]{1,0:T(8,128)(2,1)S(1)} %collective-permute-done.1), channel_id=1, source_target_pairs={{0,2},{1,3},{2,0},{3,1},{4,6},{5,7},{6,4},{7,5},{8,10},{9,11},{10,... | collective-permute-start | bytes 208904 | tf_op jit(solution)/shard_map/ppermute | solution.py:335
  13.8 4.4 %collective-permute-start.6 = (bf16[136,256]{1,0:T(8,128)(2,1)S(1)}, bf16[136,256]{1,0:T(8,128)(2,1)S(1)}, u32[]{:S(2)}, u32[]{:S(2)}) collective-permute-start(bf16[136,256]{1,0:T(8,128)(2,1)S(1)} %collective-permute-done.2), channel_id=1, source_target_pairs={{0,2},{1,3},{2,0},{3,1},{4,6},{5,7},{6,4},{7,5},{8,10},{9,11},{10,... | collective-permute-start | bytes 208904 | tf_op jit(solution)/shard_map/ppermute | solution.py:335
  15.1 6.1 %collective-permute-start.7 = (bf16[4,136,256]{2,1,0:T(8,128)(2,1)S(1)}, bf16[4,136,256]{2,1,0:T(8,128)(2,1)S(1)}, u32[]{:S(2)}, u32[]{:S(2)}) collective-permute-start(bf16[4,136,256]{2,1,0:T(8,128)(2,1)S(1)} %bitcast_dynamic-update-slice_fusion.x_ref.column_ref), channel_id=1, source_target_pairs={{0,1},{1,0},{2,3},{3,2},{4,5},{5,4},{6,7},{7,6},{8,9},{9,8},{10,11... | collective-permute-start | bytes 835592 | tf_op jit(solution)/shard_map/ppermute | solution.py:335
  18.3 4.8 %collective-permute-start.8 = (bf16[4,136,256]{2,1,0:T(8,128)(2,1)S(1)}, bf16[4,136,256]{2,1,0:T(8,128)(2,1)S(1)}, u32[]{:S(2)}, u32[]{:S(2)}) collective-permute-start(bf16[4,136,256]{2,1,0:T(8,128)(2,1)S(1)} %pad_maximum_fusion.plane_ref), channel_id=1, source_target_pairs={{0,1},{1,0},{2,3},{3,2},{4,5},{5,4},{6,7},{7,6},{8,9},{9,8},{10,11... | collective-permute-start | bytes 835592 | tf_op jit(solution)/shard_map/ppermute | solution.py:335

commit v5 on v4

--- a/solution.py
+++ b/solution.py
@@ -20,6 +20,7 @@
 SHIFTS = 2 * REACH + 1
 OUT_LANES = LAGS * CH
 BLEND = 32.0
+HEADER = 8
 GROUPS = 4
 
 VMEM = pl.BlockSpec(memory_space=pltpu.VMEM)
@@ -28,11 +29,9 @@
 HBM = pl.BlockSpec(memory_space=pltpu.HBM)
 
 
-def piece_offset(devices, index):
-    far = devices // GROUPS
-    return (
-        lax.rem(index, far) * 4 + lax.rem(lax.div(index, far), 2) * 2 + lax.div(index, 2 * far)
-    )
+def piece_index(devices, offset):
+    bits = (devices // GROUPS).bit_length() - 1
+    return (offset >> 2) | (((offset >> 1) & 1) << bits) | ((offset & 1) << (bits + 1))
 
 
 def prep_kernel(samples_ref, scales_ref, piece_ref, x_ref, s_ref, turned_ref, sem):
@@ -87,25 +86,25 @@
     for i in range(devices):
         own_bin = jnp.where(owner_ref[i] == own, i, own_bin)
 
-    def row(i, found):
+    def row(p, found):
         found = list(found)
-        p = own ^ piece_offset(devices, i)
-        for j in range(devices):
-            group = j // members
-            q = own ^ piece_offset(devices, jnp.int32(j))
-            list_ref[GROUPS + group * devices * members + found[group]] = i * devices + j
-            found[group] = found[group] + jnp.where(bins_ref[p, q] == own_bin, 1, 0)
+        cells = [bins_ref[p, q] for q in range(devices)]
+        for q, cell in enumerate(cells):
+            kind = q % GROUPS
+            list_ref[HEADER + kind * devices * members + found[kind]] = p * members + q // GROUPS
+            found[kind] = found[kind] + jnp.where(cell == own_bin, 1, 0)
         return tuple(found)
 
     found = lax.fori_loop(0, devices, row, (jnp.int32(0),) * GROUPS)
-    for group in range(GROUPS):
-        list_ref[group] = found[group]
+    list_ref[0] = own
+    for kind in range(GROUPS):
+        list_ref[1 + kind] = found[kind]
 
 
 def find_pairs(devices, own, bin_ids, owner_table):
     return pl.pallas_call(
         functools.partial(pairs_kernel, devices),
-        out_shape=jax.ShapeDtypeStruct((GROUPS + devices * devices + 1,), jnp.int32),
+        out_shape=jax.ShapeDtypeStruct((HEADER + devices * devices + 1,), jnp.int32),
         in_specs=[SMEM] * 3,
         out_specs=SMEM,
         compiler_params=pltpu.CompilerParams(vmem_limit_bytes=1 << 20),
@@ -177,31 +176,45 @@
     )(pieces)
 
 
-def add_pairs(devices, first, base, start, stop, list_ref, x_ref, sums_ref):
+def add_pairs(devices, group, list_ref, x_ref, sums_ref):
+    members = devices // GROUPS
+    own = list_ref[0]
+    kind = (own & 3) ^ (((group & 1) << 1) | (group >> 1))
+    base = HEADER + kind * devices * members
+
     def add(place, carry):
         code = list_ref[base + place]
-        i, j = lax.div(code, devices), lax.rem(code, devices) - first
+        i = piece_index(devices, own ^ (code >> (members.bit_length() - 1)))
+        j = (code & (members - 1)) ^ (own >> 2)
         scale = x_ref[j, ROWS : ROWS + 1, :].astype(jnp.float32)
         sums_ref[i] = sums_ref[i] + x_ref[j, 0:ROWS, :].astype(jnp.float32) * scale
         return carry
 
-    lax.fori_loop(start, stop, add, 0)
-
-
-def early_kernel(devices, list_ref, column_ref, side_ref, turned_ref, sums_ref, high_ref, low_ref):
-    members = devices // GROUPS
+    lax.fori_loop(0, list_ref[1 + kind], add, 0)
+
+
+def early_kernel(
+    devices, pairs_ref, column_ref, side_ref, turned_ref, sums_ref, list_ref, high_ref, low_ref, sem
+):
+    members = devices // GROUPS
+    copy = pltpu.make_async_copy(pairs_ref, list_ref, sem)
+    copy.start()
     sums_ref[...] = jnp.zeros_like(sums_ref)
     turn_group(loader(side_ref), members, turned_ref, high_ref, low_ref)
+    copy.wait()
     for group, ref in ((0, column_ref), (2, side_ref)):
-        base = GROUPS + group * devices * members
-        add_pairs(devices, group * members, base, 0, list_ref[group], list_ref, ref, sums_ref)
-
-
-def plane_kernel(devices, list_ref, plane_ref, _, turned_ref, sums_ref, high_ref, low_ref):
-    members = devices // GROUPS
+        add_pairs(devices, group, list_ref, ref, sums_ref)
+
+
+def plane_kernel(
+    devices, pairs_ref, plane_ref, _, turned_ref, sums_ref, list_ref, high_ref, low_ref, sem
+):
+    members = devices // GROUPS
+    copy = pltpu.make_async_copy(pairs_ref, list_ref, sem)
+    copy.start()
     turn_group(loader(plane_ref), members, turned_ref, high_ref, low_ref)
-    base = GROUPS + devices * members
-    add_pairs(devices, members, base, 0, list_ref[1], list_ref, plane_ref, sums_ref)
+    copy.wait()
+    add_pairs(devices, 1, list_ref, plane_ref, sums_ref)
 
 
 def early(devices, pairs, column, side):
@@ -212,11 +225,13 @@
             jax.ShapeDtypeStruct((2 * LANES, members * ROWS), jnp.bfloat16),
             jax.ShapeDtypeStruct((devices, ROWS, LANES), jnp.float32),
         ),
-        in_specs=[SMEM, VMEM, VMEM],
+        in_specs=[ANY, VMEM, VMEM],
         out_specs=(VMEM, VMEM),
         scratch_shapes=[
-            pltpu.VMEM((members * ROWS, LANES), jnp.bfloat16),
-            pltpu.VMEM((members * ROWS, LANES), jnp.bfloat16),
+            pltpu.SMEM(pairs.shape, jnp.int32),
+            pltpu.VMEM((members * ROWS, LANES), jnp.bfloat16),
+            pltpu.VMEM((members * ROWS, LANES), jnp.bfloat16),
+            pltpu.SemaphoreType.DMA,
         ],
         compiler_params=pltpu.CompilerParams(vmem_limit_bytes=(2 << 20) + devices * (1 << 19)),
         cost_estimate=pl.CostEstimate(
@@ -234,12 +249,14 @@
             jax.ShapeDtypeStruct((2 * LANES, members * ROWS), jnp.bfloat16),
             jax.ShapeDtypeStruct(sums.shape, jnp.float32),
         ),
-        in_specs=[SMEM, VMEM, VMEM],
+        in_specs=[ANY, VMEM, VMEM],
         out_specs=(VMEM, VMEM),
         input_output_aliases={2: 1},
         scratch_shapes=[
-            pltpu.VMEM((members * ROWS, LANES), jnp.bfloat16),
-            pltpu.VMEM((members * ROWS, LANES), jnp.bfloat16),
+            pltpu.SMEM(pairs.shape, jnp.int32),
+            pltpu.VMEM((members * ROWS, LANES), jnp.bfloat16),
+            pltpu.VMEM((members * ROWS, LANES), jnp.bfloat16),
+            pltpu.SemaphoreType.DMA,
         ],
         compiler_params=pltpu.CompilerParams(vmem_limit_bytes=(2 << 20) + devices * (1 << 19)),
         cost_estimate=pl.CostEstimate(
@@ -250,16 +267,17 @@
 
 
 def stack_kernel(
-    devices, span, list_ref, a0_ref, a1_ref, a2_ref, _, x_ref, out_ref, sums_ref,
-    a3_ref, high_ref, low_ref, yh_ref, yl_ref,
+    devices, span, pairs_ref, a0_ref, a1_ref, a2_ref, _, x_ref, out_ref, sums_ref,
+    list_ref, a3_ref, high_ref, low_ref, yh_ref, yl_ref, sem,
 ):
     members = devices // GROUPS
     depth = members * ROWS
     slab = members * COARSE
-    last = GROUPS - 1
-    base = GROUPS + last * devices * members
-    add_pairs(devices, last * members, base, 0, list_ref[last], list_ref, x_ref, sums_ref)
+    copy = pltpu.make_async_copy(pairs_ref, list_ref, sem)
+    copy.start()
     turn_group(loader(x_ref), members, a3_ref, high_ref, low_ref)
+    copy.wait()
+    add_pairs(devices, GROUPS - 1, list_ref, x_ref, sums_ref)
 
     def put(group, member, u1, value):
         high, low = split_right(value)
@@ -294,7 +312,7 @@
     stack = jnp.zeros((CH, OUT_LANES), jnp.float32)
     for v in range(STEP):
         stack = stack + product[CH * v : CH * (v + 1), CH * v : CH * v + OUT_LANES]
-    count = sum(list_ref[group] for group in range(GROUPS)).astype(jnp.float32)
+    count = sum(list_ref[1 + kind] for kind in range(GROUPS)).astype(jnp.float32)
     stack = stack / jnp.sqrt(jnp.full((CH, OUT_LANES), count * span, jnp.float32))
     for a in range(CH):
         out_ref[0:1, a * OUT_LANES : (a + 1) * OUT_LANES] = stack[a : a + 1]
@@ -310,15 +328,17 @@
             jax.ShapeDtypeStruct((1, CH * OUT_LANES), jnp.float32),
             jax.ShapeDtypeStruct(sums.shape, jnp.float32),
         ),
-        in_specs=[SMEM] + [VMEM] * 5,
+        in_specs=[ANY] + [VMEM] * 5,
         out_specs=(VMEM, VMEM),
         input_output_aliases={4: 1},
         scratch_shapes=[
+            pltpu.SMEM(pairs.shape, jnp.int32),
             pltpu.VMEM((2 * LANES, depth), jnp.bfloat16),
             pltpu.VMEM((depth, LANES), jnp.bfloat16),
             pltpu.VMEM((depth, LANES), jnp.bfloat16),
             pltpu.VMEM((GROUPS, extended, LANES), jnp.bfloat16),
             pltpu.VMEM((GROUPS, extended, LANES), jnp.bfloat16),
+            pltpu.SemaphoreType.DMA,
         ],
         compiler_params=pltpu.CompilerParams(vmem_limit_bytes=(8 << 20) + devices * (5 << 17)),
         name="stack",

time: 27.8 us -> 26.8 us (0.964)
  Pallas kernels: 10.9 us -> 9.83 us
    pallas_call x1, Pallas kernels: 2.59 us -> 2.17 us  [find_pairs(): pl.pallas_call(functools.partial(pairs_kernel, devices), out_shape=jax.Sh...]
    pallas_call x1, Pallas kernels: 1.04 us -> 0.69 us  [early(): pl.pallas_call(functools.partial(early_kernel, devices), out_shape=(jax.S...]
  transfers between devices with their start and end apart: 9 -> 9, of which waited for: 3 -> 3; matrix products, arithmetic and copies ran while one was open for 0% -> 0% of each run, Pallas kernels for 17% -> 14%
where the time goes in v5:
time: 26.8 us; the launch traced here: 26.6 us
  starting transfers between devices  10.7 us (40%)
  Pallas kernels  9.83 us (37%)
  waiting for transfers between devices  5.89 us (22%)
    ppermute x9, starting transfers between devices, swap(): lax.ppermute(value, 'chan', [(i, i ^ offset) for i in range(devices)])  10.7 us
    ppermute x9, waiting for transfers between devices, swap(): lax.ppermute(value, 'chan', [(i, i ^ offset) for i in range(devices)])  5.89 us
    pallas_call x1, Pallas kernels, stack_bin(): pl.pallas_call(functools.partial(stack_kernel, devices, float(span)), out...  4.46 us
    pallas_call x1, Pallas kernels, find_pairs(): pl.pallas_call(functools.partial(pairs_kernel, devices), out_shape=jax.Sh...  2.17 us
    pallas_call x1, Pallas kernels, prep(): pl.pallas_call(prep_kernel, out_shape=jax.ShapeDtypeStruct((HEAD, LANES),...  1.66 us
    pallas_call x1, Pallas kernels, early(): pl.pallas_call(functools.partial(early_kernel, devices), out_shape=(jax.S...  0.69 us
    pallas_call x1, Pallas kernels, add_plane(): pl.pallas_call(functools.partial(plane_kernel, devices), out_shape=(jax.S...  0.6 us
  transfers between devices with their start and end apart: 9, of which 3 were waited for; matrix products, arithmetic and copies ran while one was open for 0% of the time, Pallas kernels for 14%

profile of v5, /device:TPU:0, one launch (start us, length us, event | category | flops | bytes accessed | tf_op | source)
XLA Modules:
  0.0 26.6 jit_solution(17376498858175236902)
XLA Ops:
  0.0 1.7 %prep.1 = bf16[136,256]{1,0:T(8,128)(2,1)S(1)} custom-call(bf16[16,2048]{1,0:T(8,128)(2,1)} %samples_ref.1, bf16[1,16]{1,0:T(2,128)(2,1)} %bitcast.18), custom_call_target="tpu_custom_call" | custom-call | tf_op jit(solution)/shard_map/prep/pallas_call | solution.py:63
  1.7 3.1 %collective-permute-start = (bf16[136,256]{1,0:T(8,128)(2,1)S(1)}, bf16[136,256]{1,0:T(8,128)(2,1)S(1)}, u32[]{:S(2)}, u32[]{:S(2)}) collective-permute-start(bf16[136,256]{1,0:T(8,128)(2,1)S(1)} %prep.1), channel_id=1, source_target_pairs={{0,4},{1,5},{2,6},{3,7},{4,0},{5,1},{6,2},{7,3},{8,12},{9,13},{10,... | collective-permute-start | bytes 208904 | tf_op jit(solution)/shard_map/ppermute | solution.py:355
  4.8 2.6 %collective-permute-start.1 = (bf16[136,256]{1,0:T(8,128)(2,1)S(1)}, bf16[136,256]{1,0:T(8,128)(2,1)S(1)}, u32[]{:S(2)}, u32[]{:S(2)}) collective-permute-start(bf16[136,256]{1,0:T(8,128)(2,1)S(1)} %prep.1), channel_id=1, source_target_pairs={{0,8},{1,9},{2,10},{3,11},{4,12},{5,13},{6,14},{7,15},{8,0},{9,1},... | collective-permute-start | bytes 208904 | tf_op jit(solution)/shard_map/ppermute | solution.py:355
  7.4 0.0 collective-permute-start.2
  7.4 1.7 %collective-permute-start.3 = (bf16[136,256]{1,0:T(8,128)(2,1)S(1)}, bf16[136,256]{1,0:T(8,128)(2,1)S(1)}, u32[]{:S(2)}, u32[]{:S(2)}) collective-permute-start(bf16[136,256]{1,0:T(8,128)(2,1)S(1)} %prep.1), channel_id=1, source_target_pairs={{0,2},{1,3},{2,0},{3,1},{4,6},{5,7},{6,4},{7,5},{8,10},{9,11},{10,... | collective-permute-start | bytes 208904 | tf_op jit(solution)/shard_map/ppermute | solution.py:355
  9.1 0.0 collective-permute-done
  9.1 0.4 %collective-permute-start.4 = (bf16[136,256]{1,0:T(8,128)(2,1)S(1)}, bf16[136,256]{1,0:T(8,128)(2,1)S(1)}, u32[]{:S(2)}, u32[]{:S(2)}) collective-permute-start(bf16[136,256]{1,0:T(8,128)(2,1)S(1)} %collective-permute-done), channel_id=1, source_target_pairs={{0,2},{1,3},{2,0},{3,1},{4,6},{5,7},{6,4},{7,5},{8,10},{9,11},{10,... | collective-permute-start | bytes 208904 | tf_op jit(solution)/shard_map/ppermute | solution.py:355
  9.5 2.8 %collective-permute-done.1 = bf16[136,256]{1,0:T(8,128)(2,1)S(1)} collective-permute-done((bf16[136,256]{1,0:T(8,128)(2,1)S(1)}, bf16[136,256]{1,0:T(8,128)(2,1)S(1)}, u32[]{:S(2)}, u32[]{:S(2)}) %collective-permute-start.1) | collective-permute-done | bytes 69664 | tf_op jit(solution)/shard_map/ppermute | solution.py:355
  12.3 1.5 %collective-permute-start.5 = (bf16[136,256]{1,0:T(8,128)(2,1)S(1)}, bf16[136,256]{1,0:T(8,128)(2,1)S(1)}, u32[]{:S(2)}, u32[]{:S(2)}) collective-permute-start(bf16[136,256]{1,0:T(8,128)(2,1)S(1)} %collective-permute-done.1), channel_id=1, source_target_pairs={{0,2},{1,3},{2,0},{3,1},{4,6},{5,7},{6,4},{7,5},{8,10},{9,11},{10,... | collective-permute-start | bytes 208904 | tf_op jit(solution)/shard_map/ppermute | solution.py:355
  13.8 0.0 collective-permute-done.2
  13.8 1.3 %collective-permute-start.6 = (bf16[136,256]{1,0:T(8,128)(2,1)S(1)}, bf16[136,256]{1,0:T(8,128)(2,1)S(1)}, u32[]{:S(2)}, u32[]{:S(2)}) collective-permute-start(bf16[136,256]{1,0:T(8,128)(2,1)S(1)} %collective-permute-done.2), channel_id=1, source_target_pairs={{0,2},{1,3},{2,0},{3,1},{4,6},{5,7},{6,4},{7,5},{8,10},{9,11},{10,... | collective-permute-start | bytes 208904 | tf_op jit(solution)/shard_map/ppermute | solution.py:355
  15.1 0.0 collective-permute-start.7
  15.1 0.0 collective-permute-done.3
  15.1 0.0 collective-permute-done.4
  15.1 1.5 %collective-permute-done.5 = bf16[136,256]{1,0:T(8,128)(2,1)S(1)} collective-permute-done((bf16[136,256]{1,0:T(8,128)(2,1)S(1)}, bf16[136,256]{1,0:T(8,128)(2,1)S(1)}, u32[]{:S(2)}, u32[]{:S(2)}) %collective-permute-start.5) | collective-permute-done | bytes 69664 | tf_op jit(solution)/shard_map/ppermute | solution.py:355
  16.6 1.6 %collective-permute-done.6 = bf16[136,256]{1,0:T(8,128)(2,1)S(1)} collective-permute-done((bf16[136,256]{1,0:T(8,128)(2,1)S(1)}, bf16[136,256]{1,0:T(8,128)(2,1)S(1)}, u32[]{:S(2)}, u32[]{:S(2)}) %collective-permute-start.6) | collective-permute-done | bytes 69664 | tf_op jit(solution)/shard_map/ppermute | solution.py:355
  18.3 0.1 collective-permute-start.8
  18.3 2.2 %pairs.1.pairs_ref = s32[265]{0:T(512)S(1)} custom-call(s32[1]{0:T(128)} %bitcast.own_ref, s32[16,16]{1,0:T(8,128)} %bins_ref.1, s32[16]{0:T(128)} %owner_ref.1), custom_call_target="tpu_custom_call" | custom-call | flops 10000000 | bytes 1048576 | tf_op jit(solution)/shard_map/pairs/pallas_call | solution.py:105
  20.5 0.3 turn.1.a0_ref
  20.8 0.0 collective-permute-done.7.side_ref
  20.8 0.7 %early.1 = (bf16[512,512]{1,0:T(8,128)(2,1)S(1)}, f32[16,128,256]{2,1,0:T(8,128)S(1)}) custom-call(s32[265]{0:T(512)S(1)} %pairs.1.pairs_ref, bf16[4,136,256]{2,1,0:T(8,128)(2,1)S(1)} %bitcast_dynamic-update-slice_fusion.x_ref.column_ref, bf16[4,136,256]{2,1,0:T(8,128)(2,1)S(1)} %collective-permute-done.7.side_ref), custom_call_target="tpu_custom_call" | custom-call | flops 32000000 | bytes 4194304 | tf_op jit(solution)/shard_map/early/pallas_call | solution.py:222
  21.5 0.6 %plane.1 = (bf16[512,512]{1,0:T(8,128)(2,1)S(1)}, f32[16,128,256]{2,1,0:T(8,128)S(1)}) custom-call(s32[265]{0:T(512)S(1)} %pairs.1.pairs_ref, bf16[4,136,256]{2,1,0:T(8,128)(2,1)S(1)} %pad_maximum_fusion.plane_ref, f32[16,128,256]{2,1,0:T(8,128)S(1)} %get-tuple-element.58._), custom_call_target="tpu_custom_call", output_to_operand_aliasing={{1}: (2, {})} | custom-call | flops 16000000 | bytes 2097152 | tf_op jit(solution)/shard_map/plane/pallas_call | solution.py:246
  22.1 0.0 collective-permute-done.8.x_ref
  22.1 4.5 %stack.21 = (f32[1,16640]{1,0:T(1,128)}, f32[16,128,256]{2,1,0:T(8,128)S(1)}) custom-call(s32[265]{0:T(512)S(1)} %pairs.1.pairs_ref, bf16[512,512]{1,0:T(8,128)(2,1)S(1)} %turn.1.a0_ref, bf16[512,512]{1,0:T(8,128)(2,1)S(1)} %get-tuple-element.59.a1_ref, bf16[512,512]{1,0:T(8,128)(2,1)S(1)} %get-tuple-element.60.a2_ref, ...), custom_call_target="tpu_custom_call", output_to_operand_aliasing={{1}: (4, {})} | custom-call | tf_op jit(solution)/shard_map/stack/pallas_call | solution.py:325
  (5 shorter events, 0.1 us)
Async XLA Ops:
  1.7 7.5 %collective-permute-start = (bf16[136,256]{1,0:T(8,128)(2,1)S(1)}, bf16[136,256]{1,0:T(8,128)(2,1)S(1)}, u32[]{:S(2)}, u32[]{:S(2)}) collective-permute-start(bf16[136,256]{1,0:T(8,128)(2,1)S(1)} %prep.1), channel_id=1, source_target_pairs={{0,4},{1,5},{2,6},{3,7},{4,0},{5,1},{6,2},{7,3},{8,12},{9,13},{10,... | collective-permute-start | bytes 208904 | tf_op jit(solution)/shard_map/ppermute | solution.py:355
  4.8 7.5 %collective-permute-start.1 = (bf16[136,256]{1,0:T(8,128)(2,1)S(1)}, bf16[136,256]{1,0:T(8,128)(2,1)S(1)}, u32[]{:S(2)}, u32[]{:S(2)}) collective-permute-start(bf16[136,256]{1,0:T(8,128)(2,1)S(1)} %prep.1), channel_id=1, source_target_pairs={{0,8},{1,9},{2,10},{3,11},{4,12},{5,13},{6,14},{7,15},{8,0},{9,1},... | collective-permute-start | bytes 208904 | tf_op jit(solution)/shard_map/ppermute | solution.py:355
  7.4 6.5 %collective-permute-start.2 = (bf16[136,256]{1,0:T(8,128)(2,1)S(1)}, bf16[136,256]{1,0:T(8,128)(2,1)S(1)}, u32[]{:S(2)}, u32[]{:S(2)}) collective-permute-start(bf16[136,256]{1,0:T(8,128)(2,1)S(1)} %prep.1), channel_id=1, source_target_pairs={{0,12},{1,13},{2,14},{3,15},{4,8},{5,9},{6,10},{7,11},{8,4},{9,5},... | collective-permute-start | bytes 208904 | tf_op jit(solution)/shard_map/ppermute | solution.py:355
  7.4 7.7 %collective-permute-start.3 = (bf16[136,256]{1,0:T(8,128)(2,1)S(1)}, bf16[136,256]{1,0:T(8,128)(2,1)S(1)}, u32[]{:S(2)}, u32[]{:S(2)}) collective-permute-start(bf16[136,256]{1,0:T(8,128)(2,1)S(1)} %prep.1), channel_id=1, source_target_pairs={{0,2},{1,3},{2,0},{3,1},{4,6},{5,7},{6,4},{7,5},{8,10},{9,11},{10,... | collective-permute-start | bytes 208904 | tf_op jit(solution)/shard_map/ppermute | solution.py:355
  9.1 6.0 %collective-permute-start.4 = (bf16[136,256]{1,0:T(8,128)(2,1)S(1)}, bf16[136,256]{1,0:T(8,128)(2,1)S(1)}, u32[]{:S(2)}, u32[]{:S(2)}) collective-permute-start(bf16[136,256]{1,0:T(8,128)(2,1)S(1)} %collective-permute-done), channel_id=1, source_target_pairs={{0,2},{1,3},{2,0},{3,1},{4,6},{5,7},{6,4},{7,5},{8,10},{9,11},{10,... | collective-permute-start | bytes 208904 | tf_op jit(solution)/shard_map/ppermute | solution.py:355
  12.3 4.3 %collective-permute-start.5 = (bf16[136,256]{1,0:T(8,128)(2,1)S(1)}, bf16[136,256]{1,0:T(8,128)(2,1)S(1)}, u32[]{:S(2)}, u32[]{:S(2)}) collective-permute-start(bf16[136,256]{1,0:T(8,128)(2,1)S(1)} %collective-permute-done.1), channel_id=1, source_target_pairs={{0,2},{1,3},{2,0},{3,1},{4,6},{5,7},{6,4},{7,5},{8,10},{9,11},{10,... | collective-permute-start | bytes 208904 | tf_op jit(solution)/shard_map/ppermute | solution.py:355
  13.8 4.4 %collective-permute-start.6 = (bf16[136,256]{1,0:T(8,128)(2,1)S(1)}, bf16[136,256]{1,0:T(8,128)(2,1)S(1)}, u32[]{:S(2)}, u32[]{:S(2)}) collective-permute-start(bf16[136,256]{1,0:T(8,128)(2,1)S(1)} %collective-permute-done.2), channel_id=1, source_target_pairs={{0,2},{1,3},{2,0},{3,1},{4,6},{5,7},{6,4},{7,5},{8,10},{9,11},{10,... | collective-permute-start | bytes 208904 | tf_op jit(solution)/shard_map/ppermute | solution.py:355
  15.1 5.7 %collective-permute-start.7 = (bf16[4,136,256]{2,1,0:T(8,128)(2,1)S(1)}, bf16[4,136,256]{2,1,0:T(8,128)(2,1)S(1)}, u32[]{:S(2)}, u32[]{:S(2)}) collective-permute-start(bf16[4,136,256]{2,1,0:T(8,128)(2,1)S(1)} %bitcast_dynamic-update-slice_fusion.x_ref.column_ref), channel_id=1, source_target_pairs={{0,1},{1,0},{2,3},{3,2},{4,5},{5,4},{6,7},{7,6},{8,9},{9,8},{10,11... | collective-permute-start | bytes 835592 | tf_op jit(solution)/shard_map/ppermute | solution.py:355
  18.3 3.8 %collective-permute-start.8 = (bf16[4,136,256]{2,1,0:T(8,128)(2,1)S(1)}, bf16[4,136,256]{2,1,0:T(8,128)(2,1)S(1)}, u32[]{:S(2)}, u32[]{:S(2)}) collective-permute-start(bf16[4,136,256]{2,1,0:T(8,128)(2,1)S(1)} %pad_maximum_fusion.plane_ref), channel_id=1, source_target_pairs={{0,1},{1,0},{2,3},{3,2},{4,5},{5,4},{6,7},{7,6},{8,9},{9,8},{10,11... | collective-permute-start | bytes 835592 | tf_op jit(solution)/shard_map/ppermute | solution.py:355

commit v6 on v5

--- a/solution.py
+++ b/solution.py
@@ -34,7 +34,7 @@
     return (offset >> 2) | (((offset >> 1) & 1) << bits) | ((offset & 1) << (bits + 1))
 
 
-def prep_kernel(samples_ref, scales_ref, piece_ref, x_ref, s_ref, turned_ref, sem):
+def prep_kernel(samples_ref, scales_ref, piece_ref, x_ref, s_ref, turned_ref, rows_ref, sem):
     copies = [
         pltpu.make_async_copy(samples_ref, x_ref, sem.at[0]),
         pltpu.make_async_copy(scales_ref, s_ref, sem.at[1]),
@@ -43,15 +43,29 @@
         copy.start()
     copies[0].wait()
     samples = x_ref[...].astype(jnp.float32)
-    for u2 in range(COARSE):
-        turned_ref[u2 * 128 : (u2 + 1) * 128, 0:CH] = samples[:, u2 * 128 : (u2 + 1) * 128].T
-    for u1 in range(FINE):
-        parts = [
-            turned_ref[pl.ds(STEP * u1 + v, COARSE, stride=128), 0:CH] for v in range(STEP)
+    granule = lax.broadcasted_iota(jnp.int32, (FINE, 128), 1) // CH
+    for half in range(2):
+        stripes = [
+            samples[:, u2 * 128 : (u2 + 1) * 128] for u2 in range(8 * half, 8 * half + 8)
         ]
-        piece_ref[u1 * COARSE : (u1 + 1) * COARSE, :] = jnp.concatenate(parts, axis=1).astype(
-            jnp.bfloat16
-        )
+        turned_ref[half] = jnp.concatenate(stripes, axis=0).T
+    for half in range(2):
+        for part in range(2):
+            tiles = [
+                turned_ref[half, pl.ds(8 * part + k, FINE, stride=STEP), :] for k in range(8)
+            ]
+            for step in (1, 2, 4):
+                upper = (granule & step) != 0
+                for k in range(8):
+                    if k & step:
+                        continue
+                    one, two = tiles[k], tiles[k + step]
+                    tiles[k] = jnp.where(upper, pltpu.roll(two, CH * step, 1), one)
+                    tiles[k + step] = jnp.where(upper, two, pltpu.roll(one, 128 - CH * step, 1))
+            for k in range(8):
+                rows_ref[part, pl.ds(8 * half + k, FINE, stride=COARSE), :] = tiles[k]
+    for part in range(2):
+        piece_ref[0:ROWS, part * 128 : (part + 1) * 128] = rows_ref[part].astype(jnp.bfloat16)
     copies[1].wait()
     scales = s_ref[...].astype(jnp.float32)
     piece_ref[ROWS:HEAD, :] = jnp.broadcast_to(
@@ -68,7 +82,8 @@
         scratch_shapes=[
             pltpu.VMEM(samples.shape, jnp.bfloat16),
             pltpu.VMEM((1, CH), jnp.bfloat16),
-            pltpu.VMEM((COARSE * 128, 128), jnp.float32),
+            pltpu.VMEM((2, 128, 128), jnp.float32),
+            pltpu.VMEM((2, ROWS, 128), jnp.float32),
             pltpu.SemaphoreType.DMA((2,)),
         ],
         compiler_params=pltpu.CompilerParams(vmem_limit_bytes=4 << 20),
@@ -364,8 +379,9 @@
         plane.append(swap(one, 2))
         own_column = own_column.at[i].set(one)
     side_column = swap(own_column, 1)
-    own_plane = jnp.stack(plane)
-    side_plane = swap(own_plane, 1)
+    first_rows = jnp.stack(plane[:-1])
+    side_plane = jnp.concatenate([swap(first_rows, 1), swap(plane[-1], 1)[None]])
+    own_plane = jnp.concatenate([first_rows, plane[-1][None]])
     turned_0 = turn(own_column)
     turned_2, sums = early(devices, pairs, own_column, side_column)
     turned_1, sums = add_plane(devices, pairs, own_plane, sums)

time: 26.8 us -> 27.1 us (1.011)
  Pallas kernels: 9.83 us -> 9.5 us
  starting transfers between devices: 10.7 us -> 11 us
    ppermute x9 -> x10, starting transfers between devices: 10.7 us -> 11 us  [swap(): lax.ppermute(value, 'chan', [(i, i ^ offset) for i in range(devices)])]
    pallas_call x1, Pallas kernels: 1.66 us -> 1.33 us  [prep(): pl.pallas_call(prep_kernel, out_shape=jax.ShapeDtypeStruct((HEAD, LANES),...]
    ppermute x9 -> x10, waiting for transfers between devices: 5.89 us -> 6.05 us  [swap(): lax.ppermute(value, 'chan', [(i, i ^ offset) for i in range(devices)])]
  transfers between devices with their start and end apart: 9 -> 10, of which waited for: 3 -> 3; matrix products, arithmetic and copies ran while one was open for 0% -> 0% of each run, Pallas kernels for 14% -> 14%
where the time goes in v6:
time: 27.1 us; the launch traced here: 26.9 us
  starting transfers between devices  11 us (41%)
  Pallas kernels  9.5 us (35%)
  waiting for transfers between devices  6.05 us (22%)
    ppermute x10, starting transfers between devices, swap(): lax.ppermute(value, 'chan', [(i, i ^ offset) for i in range(devices)])  11 us
    ppermute x10, waiting for transfers between devices, swap(): lax.ppermute(value, 'chan', [(i, i ^ offset) for i in range(devices)])  6.05 us
    pallas_call x1, Pallas kernels, stack_bin(): pl.pallas_call(functools.partial(stack_kernel, devices, float(span)), out...  4.45 us
    pallas_call x1, Pallas kernels, find_pairs(): pl.pallas_call(functools.partial(pairs_kernel, devices), out_shape=jax.Sh...  2.17 us
    pallas_call x1, Pallas kernels, prep(): pl.pallas_call(prep_kernel, out_shape=jax.ShapeDtypeStruct((HEAD, LANES),...  1.33 us
    pallas_call x1, Pallas kernels, early(): pl.pallas_call(functools.partial(early_kernel, devices), out_shape=(jax.S...  0.69 us
    pallas_call x1, Pallas kernels, add_plane(): pl.pallas_call(functools.partial(plane_kernel, devices), out_shape=(jax.S...  0.61 us
  transfers between devices with their start and end apart: 10, of which 3 were waited for; matrix products, arithmetic and copies ran while one was open for 0% of the time, Pallas kernels for 14%

profile of v6, /device:TPU:0, one launch (start us, length us, event | category | flops | bytes accessed | tf_op | source)
XLA Modules:
  0.0 26.9 jit_solution(8546030223727454250)
XLA Ops:
  0.0 1.3 %prep.1 = bf16[136,256]{1,0:T(8,128)(2,1)S(1)} custom-call(bf16[16,2048]{1,0:T(8,128)(2,1)} %samples_ref.1, bf16[1,16]{1,0:T(2,128)(2,1)} %bitcast.23), custom_call_target="tpu_custom_call" | custom-call | tf_op jit(solution)/shard_map/prep/pallas_call | solution.py:77
  1.3 3.1 %collective-permute-start = (bf16[136,256]{1,0:T(8,128)(2,1)S(1)}, bf16[136,256]{1,0:T(8,128)(2,1)S(1)}, u32[]{:S(2)}, u32[]{:S(2)}) collective-permute-start(bf16[136,256]{1,0:T(8,128)(2,1)S(1)} %prep.1), channel_id=1, source_target_pairs={{0,4},{1,5},{2,6},{3,7},{4,0},{5,1},{6,2},{7,3},{8,12},{9,13},{10,... | collective-permute-start | bytes 208904 | tf_op jit(solution)/shard_map/ppermute | solution.py:370
  4.5 2.6 %collective-permute-start.1 = (bf16[136,256]{1,0:T(8,128)(2,1)S(1)}, bf16[136,256]{1,0:T(8,128)(2,1)S(1)}, u32[]{:S(2)}, u32[]{:S(2)}) collective-permute-start(bf16[136,256]{1,0:T(8,128)(2,1)S(1)} %prep.1), channel_id=1, source_target_pairs={{0,8},{1,9},{2,10},{3,11},{4,12},{5,13},{6,14},{7,15},{8,0},{9,1},... | collective-permute-start | bytes 208904 | tf_op jit(solution)/shard_map/ppermute | solution.py:370
  7.0 0.0 collective-permute-start.2
  7.1 1.7 %collective-permute-start.3 = (bf16[136,256]{1,0:T(8,128)(2,1)S(1)}, bf16[136,256]{1,0:T(8,128)(2,1)S(1)}, u32[]{:S(2)}, u32[]{:S(2)}) collective-permute-start(bf16[136,256]{1,0:T(8,128)(2,1)S(1)} %prep.1), channel_id=1, source_target_pairs={{0,2},{1,3},{2,0},{3,1},{4,6},{5,7},{6,4},{7,5},{8,10},{9,11},{10,... | collective-permute-start | bytes 208904 | tf_op jit(solution)/shard_map/ppermute | solution.py:370
  8.8 0.0 collective-permute-done
  8.8 0.4 %collective-permute-start.4 = (bf16[136,256]{1,0:T(8,128)(2,1)S(1)}, bf16[136,256]{1,0:T(8,128)(2,1)S(1)}, u32[]{:S(2)}, u32[]{:S(2)}) collective-permute-start(bf16[136,256]{1,0:T(8,128)(2,1)S(1)} %collective-permute-done), channel_id=1, source_target_pairs={{0,2},{1,3},{2,0},{3,1},{4,6},{5,7},{6,4},{7,5},{8,10},{9,11},{10,... | collective-permute-start | bytes 208904 | tf_op jit(solution)/shard_map/ppermute | solution.py:370
  9.2 2.8 %collective-permute-done.1 = bf16[136,256]{1,0:T(8,128)(2,1)S(1)} collective-permute-done((bf16[136,256]{1,0:T(8,128)(2,1)S(1)}, bf16[136,256]{1,0:T(8,128)(2,1)S(1)}, u32[]{:S(2)}, u32[]{:S(2)}) %collective-permute-start.1) | collective-permute-done | bytes 69664 | tf_op jit(solution)/shard_map/ppermute | solution.py:370
  12.0 1.5 %collective-permute-start.5 = (bf16[136,256]{1,0:T(8,128)(2,1)S(1)}, bf16[136,256]{1,0:T(8,128)(2,1)S(1)}, u32[]{:S(2)}, u32[]{:S(2)}) collective-permute-start(bf16[136,256]{1,0:T(8,128)(2,1)S(1)} %collective-permute-done.1), channel_id=1, source_target_pairs={{0,2},{1,3},{2,0},{3,1},{4,6},{5,7},{6,4},{7,5},{8,10},{9,11},{10,... | collective-permute-start | bytes 208904 | tf_op jit(solution)/shard_map/ppermute | solution.py:370
  13.5 0.0 collective-permute-done.2
  13.5 0.1 collective-permute-start.7
  13.6 0.0 collective-permute-done.3
  13.6 0.0 collective-permute-done.4
  13.6 2.7 %collective-permute-done.5 = bf16[136,256]{1,0:T(8,128)(2,1)S(1)} collective-permute-done((bf16[136,256]{1,0:T(8,128)(2,1)S(1)}, bf16[136,256]{1,0:T(8,128)(2,1)S(1)}, u32[]{:S(2)}, u32[]{:S(2)}) %collective-permute-start.5) | collective-permute-done | bytes 69664 | tf_op jit(solution)/shard_map/ppermute | solution.py:370
  16.3 0.1 collective-permute-start.8
  16.4 1.6 %collective-permute-start.6 = (bf16[136,256]{1,0:T(8,128)(2,1)S(1)}, bf16[136,256]{1,0:T(8,128)(2,1)S(1)}, u32[]{:S(2)}, u32[]{:S(2)}) collective-permute-start(bf16[136,256]{1,0:T(8,128)(2,1)S(1)} %collective-permute-done.2), channel_id=1, source_target_pairs={{0,2},{1,3},{2,0},{3,1},{4,6},{5,7},{6,4},{7,5},{8,10},{9,11},{10,... | collective-permute-start | bytes 208904 | tf_op jit(solution)/shard_map/ppermute | solution.py:370
  18.0 2.2 %pairs.1.pairs_ref = s32[265]{0:T(512)S(1)} custom-call(s32[1]{0:T(128)} %bitcast.own_ref, s32[16,16]{1,0:T(8,128)} %bins_ref.1, s32[16]{0:T(128)} %owner_ref.1), custom_call_target="tpu_custom_call" | custom-call | flops 10000000 | bytes 1048576 | tf_op jit(solution)/shard_map/pairs/pallas_call | solution.py:120
  20.2 0.3 turn.1.a0_ref
  20.4 0.6 %collective-permute-done.6 = bf16[136,256]{1,0:T(8,128)(2,1)S(1)} collective-permute-done((bf16[136,256]{1,0:T(8,128)(2,1)S(1)}, bf16[136,256]{1,0:T(8,128)(2,1)S(1)}, u32[]{:S(2)}, u32[]{:S(2)}) %collective-permute-start.6) | collective-permute-done | bytes 69664 | tf_op jit(solution)/shard_map/ppermute | solution.py:370
  21.0 0.0 collective-permute-start.9
  21.0 0.0 collective-permute-done.7.side_ref
  21.0 0.7 %early.1 = (bf16[512,512]{1,0:T(8,128)(2,1)S(1)}, f32[16,128,256]{2,1,0:T(8,128)S(1)}) custom-call(s32[265]{0:T(512)S(1)} %pairs.1.pairs_ref, bf16[4,136,256]{2,1,0:T(8,128)(2,1)S(1)} %bitcast_dynamic-update-slice_fusion.x_ref.column_ref, bf16[4,136,256]{2,1,0:T(8,128)(2,1)S(1)} %collective-permute-done.7.side_ref), custom_call_target="tpu_custom_call" | custom-call | flops 32000000 | bytes 4194304 | tf_op jit(solution)/shard_map/early/pallas_call | solution.py:237
  21.7 0.6 %plane.1 = (bf16[512,512]{1,0:T(8,128)(2,1)S(1)}, f32[16,128,256]{2,1,0:T(8,128)S(1)}) custom-call(s32[265]{0:T(512)S(1)} %pairs.1.pairs_ref, bf16[4,136,256]{2,1,0:T(8,128)(2,1)S(1)} %pad_maximum_fusion.plane_ref, f32[16,128,256]{2,1,0:T(8,128)S(1)} %get-tuple-element.58._), custom_call_target="tpu_custom_call", output_to_operand_aliasing={{1}: (2, {})} | custom-call | flops 16000000 | bytes 2097152 | tf_op jit(solution)/shard_map/plane/pallas_call | solution.py:261
  22.3 0.0 collective-permute-done.9
  22.4 0.0 collective-permute-done.8
  22.4 4.5 %stack.17 = (f32[1,16640]{1,0:T(1,128)}, f32[16,128,256]{2,1,0:T(8,128)S(1)}) custom-call(s32[265]{0:T(512)S(1)} %pairs.1.pairs_ref, bf16[512,512]{1,0:T(8,128)(2,1)S(1)} %turn.1.a0_ref, bf16[512,512]{1,0:T(8,128)(2,1)S(1)} %get-tuple-element.59.a1_ref, bf16[512,512]{1,0:T(8,128)(2,1)S(1)} %get-tuple-element.60.a2_ref, ...), custom_call_target="tpu_custom_call", output_to_operand_aliasing={{1}: (4, {})} | custom-call | tf_op jit(solution)/shard_map/stack/pallas_call | solution.py:340
  (7 shorter events, 0.1 us)
Async XLA Ops:
  1.3 7.5 %collective-permute-start = (bf16[136,256]{1,0:T(8,128)(2,1)S(1)}, bf16[136,256]{1,0:T(8,128)(2,1)S(1)}, u32[]{:S(2)}, u32[]{:S(2)}) collective-permute-start(bf16[136,256]{1,0:T(8,128)(2,1)S(1)} %prep.1), channel_id=1, source_target_pairs={{0,4},{1,5},{2,6},{3,7},{4,0},{5,1},{6,2},{7,3},{8,12},{9,13},{10,... | collective-permute-start | bytes 208904 | tf_op jit(solution)/shard_map/ppermute | solution.py:370
  4.5 7.5 %collective-permute-start.1 = (bf16[136,256]{1,0:T(8,128)(2,1)S(1)}, bf16[136,256]{1,0:T(8,128)(2,1)S(1)}, u32[]{:S(2)}, u32[]{:S(2)}) collective-permute-start(bf16[136,256]{1,0:T(8,128)(2,1)S(1)} %prep.1), channel_id=1, source_target_pairs={{0,8},{1,9},{2,10},{3,11},{4,12},{5,13},{6,14},{7,15},{8,0},{9,1},... | collective-permute-start | bytes 208904 | tf_op jit(solution)/shard_map/ppermute | solution.py:370
  7.0 6.5 %collective-permute-start.2 = (bf16[136,256]{1,0:T(8,128)(2,1)S(1)}, bf16[136,256]{1,0:T(8,128)(2,1)S(1)}, u32[]{:S(2)}, u32[]{:S(2)}) collective-permute-start(bf16[136,256]{1,0:T(8,128)(2,1)S(1)} %prep.1), channel_id=1, source_target_pairs={{0,12},{1,13},{2,14},{3,15},{4,8},{5,9},{6,10},{7,11},{8,4},{9,5},... | collective-permute-start | bytes 208904 | tf_op jit(solution)/shard_map/ppermute | solution.py:370
  7.1 6.6 %collective-permute-start.3 = (bf16[136,256]{1,0:T(8,128)(2,1)S(1)}, bf16[136,256]{1,0:T(8,128)(2,1)S(1)}, u32[]{:S(2)}, u32[]{:S(2)}) collective-permute-start(bf16[136,256]{1,0:T(8,128)(2,1)S(1)} %prep.1), channel_id=1, source_target_pairs={{0,2},{1,3},{2,0},{3,1},{4,6},{5,7},{6,4},{7,5},{8,10},{9,11},{10,... | collective-permute-start | bytes 208904 | tf_op jit(solution)/shard_map/ppermute | solution.py:370
  8.8 4.8 %collective-permute-start.4 = (bf16[136,256]{1,0:T(8,128)(2,1)S(1)}, bf16[136,256]{1,0:T(8,128)(2,1)S(1)}, u32[]{:S(2)}, u32[]{:S(2)}) collective-permute-start(bf16[136,256]{1,0:T(8,128)(2,1)S(1)} %collective-permute-done), channel_id=1, source_target_pairs={{0,2},{1,3},{2,0},{3,1},{4,6},{5,7},{6,4},{7,5},{8,10},{9,11},{10,... | collective-permute-start | bytes 208904 | tf_op jit(solution)/shard_map/ppermute | solution.py:370
  12.0 4.3 %collective-permute-start.5 = (bf16[136,256]{1,0:T(8,128)(2,1)S(1)}, bf16[136,256]{1,0:T(8,128)(2,1)S(1)}, u32[]{:S(2)}, u32[]{:S(2)}) collective-permute-start(bf16[136,256]{1,0:T(8,128)(2,1)S(1)} %collective-permute-done.1), channel_id=1, source_target_pairs={{0,2},{1,3},{2,0},{3,1},{4,6},{5,7},{6,4},{7,5},{8,10},{9,11},{10,... | collective-permute-start | bytes 208904 | tf_op jit(solution)/shard_map/ppermute | solution.py:370
  13.5 7.5 %collective-permute-start.7 = (bf16[4,136,256]{2,1,0:T(8,128)(2,1)S(1)}, bf16[4,136,256]{2,1,0:T(8,128)(2,1)S(1)}, u32[]{:S(2)}, u32[]{:S(2)}) collective-permute-start(bf16[4,136,256]{2,1,0:T(8,128)(2,1)S(1)} %bitcast_dynamic-update-slice_fusion.x_ref.column_ref), channel_id=1, source_target_pairs={{0,1},{1,0},{2,3},{3,2},{4,5},{5,4},{6,7},{7,6},{8,9},{9,8},{10,11... | collective-permute-start | bytes 835592 | tf_op jit(solution)/shard_map/ppermute | solution.py:370
  16.3 6.0 %collective-permute-start.8 = (bf16[3,136,256]{2,1,0:T(8,128)(2,1)S(1)}, bf16[3,136,256]{2,1,0:T(8,128)(2,1)S(1)}, u32[]{:S(2)}, u32[]{:S(2)}) collective-permute-start(bf16[3,136,256]{2,1,0:T(8,128)(2,1)S(1)} %pad_maximum_fusion.2), channel_id=1, source_target_pairs={{0,1},{1,0},{2,3},{3,2},{4,5},{5,4},{6,7},{7,6},{8,9},{9,8},{10,11... | collective-permute-start | bytes 626696 | tf_op jit(solution)/shard_map/ppermute | solution.py:370
  16.4 4.6 %collective-permute-start.6 = (bf16[136,256]{1,0:T(8,128)(2,1)S(1)}, bf16[136,256]{1,0:T(8,128)(2,1)S(1)}, u32[]{:S(2)}, u32[]{:S(2)}) collective-permute-start(bf16[136,256]{1,0:T(8,128)(2,1)S(1)} %collective-permute-done.2), channel_id=1, source_target_pairs={{0,2},{1,3},{2,0},{3,1},{4,6},{5,7},{6,4},{7,5},{8,10},{9,11},{10,... | collective-permute-start | bytes 208904 | tf_op jit(solution)/shard_map/ppermute | solution.py:370
  21.0 1.4 %collective-permute-start.9 = (bf16[136,256]{1,0:T(8,128)(2,1)S(1)}, bf16[136,256]{1,0:T(8,128)(2,1)S(1)}, u32[]{:S(2)}, u32[]{:S(2)}) collective-permute-start(bf16[136,256]{1,0:T(8,128)(2,1)S(1)} %collective-permute-done.6), channel_id=1, source_target_pairs={{0,1},{1,0},{2,3},{3,2},{4,5},{5,4},{6,7},{7,6},{8,9},{9,8},{10,11... | collective-permute-start | bytes 208904 | tf_op jit(solution)/shard_map/ppermute | solution.py:370

commit v7 on v6

--- a/solution.py
+++ b/solution.py
@@ -375,10 +375,14 @@
     own_column = jnp.zeros((members,) + piece.shape, piece.dtype).at[0].set(piece)
     plane = [swap(piece, 2)]
     for i in range(1, members):
-        one = swap(piece, 4 * i)
-        plane.append(swap(one, 2))
+        cross = int(i == members - 1)
+        one = swap(piece, 4 * i + cross)
+        plane.append(swap(one, 2 + cross))
         own_column = own_column.at[i].set(one)
     side_column = swap(own_column, 1)
+    crossed = own_column[members - 1]
+    own_column = own_column.at[members - 1].set(side_column[members - 1])
+    side_column = side_column.at[members - 1].set(crossed)
     first_rows = jnp.stack(plane[:-1])
     side_plane = jnp.concatenate([swap(first_rows, 1), swap(plane[-1], 1)[None]])
     own_plane = jnp.concatenate([first_rows, plane[-1][None]])

time: 27.1 us -> 25.8 us (0.952)
  waiting for transfers between devices: 6.05 us -> 4.25 us
  starting transfers between devices: 11 us -> 11.6 us
    ppermute x10, waiting for transfers between devices: 6.05 us -> 4.25 us  [swap(): lax.ppermute(value, 'chan', [(i, i ^ offset) for i in range(devices)])]
    ppermute x10, starting transfers between devices: 11 us -> 11.6 us  [swap(): lax.ppermute(value, 'chan', [(i, i ^ offset) for i in range(devices)])]
  transfers between devices with their start and end apart: 10 -> 10, of which waited for: 3 -> 3; matrix products, arithmetic and copies ran while one was open for 0% -> 0% of each run, Pallas kernels for 14% -> 15%
where the time goes in v7:
time: 25.8 us; the launch traced here: 25.6 us
  starting transfers between devices  11.6 us (45%)
  Pallas kernels  9.5 us (37%)
  waiting for transfers between devices  4.25 us (16%)
    ppermute x10, starting transfers between devices, swap(): lax.ppermute(value, 'chan', [(i, i ^ offset) for i in range(devices)])  11.6 us
    pallas_call x1, Pallas kernels, stack_bin(): pl.pallas_call(functools.partial(stack_kernel, devices, float(span)), out...  4.46 us
    ppermute x10, waiting for transfers between devices, swap(): lax.ppermute(value, 'chan', [(i, i ^ offset) for i in range(devices)])  4.25 us
    pallas_call x1, Pallas kernels, find_pairs(): pl.pallas_call(functools.partial(pairs_kernel, devices), out_shape=jax.Sh...  2.17 us
    pallas_call x1, Pallas kernels, prep(): pl.pallas_call(prep_kernel, out_shape=jax.ShapeDtypeStruct((HEAD, LANES),...  1.33 us
    pallas_call x1, Pallas kernels, early(): pl.pallas_call(functools.partial(early_kernel, devices), out_shape=(jax.S...  0.69 us
    pallas_call x1, Pallas kernels, add_plane(): pl.pallas_call(functools.partial(plane_kernel, devices), out_shape=(jax.S...  0.61 us
  transfers between devices with their start and end apart: 10, of which 3 were waited for; matrix products, arithmetic and copies ran while one was open for 0% of the time, Pallas kernels for 15%

profile of v7, /device:TPU:0, one launch (start us, length us, event | category | flops | bytes accessed | tf_op | source)
XLA Modules:
  0.0 25.6 jit_solution(16474772698588635687)
XLA Ops:
  0.0 1.3 %prep.1 = bf16[136,256]{1,0:T(8,128)(2,1)S(1)} custom-call(bf16[16,2048]{1,0:T(8,128)(2,1)} %samples_ref.1, bf16[1,16]{1,0:T(2,128)(2,1)} %bitcast.24), custom_call_target="tpu_custom_call" | custom-call | tf_op jit(solution)/shard_map/prep/pallas_call | solution.py:77
  1.3 3.1 %collective-permute-start = (bf16[136,256]{1,0:T(8,128)(2,1)S(1)}, bf16[136,256]{1,0:T(8,128)(2,1)S(1)}, u32[]{:S(2)}, u32[]{:S(2)}) collective-permute-start(bf16[136,256]{1,0:T(8,128)(2,1)S(1)} %prep.1), channel_id=1, source_target_pairs={{0,4},{1,5},{2,6},{3,7},{4,0},{5,1},{6,2},{7,3},{8,12},{9,13},{10,... | collective-permute-start | bytes 208904 | tf_op jit(solution)/shard_map/ppermute | solution.py:370
  4.5 2.6 %collective-permute-start.1 = (bf16[136,256]{1,0:T(8,128)(2,1)S(1)}, bf16[136,256]{1,0:T(8,128)(2,1)S(1)}, u32[]{:S(2)}, u32[]{:S(2)}) collective-permute-start(bf16[136,256]{1,0:T(8,128)(2,1)S(1)} %prep.1), channel_id=1, source_target_pairs={{0,8},{1,9},{2,10},{3,11},{4,12},{5,13},{6,14},{7,15},{8,0},{9,1},... | collective-permute-start | bytes 208904 | tf_op jit(solution)/shard_map/ppermute | solution.py:370
  7.0 0.0 collective-permute-start.2
  7.1 1.5 %collective-permute-start.4 = (bf16[136,256]{1,0:T(8,128)(2,1)S(1)}, bf16[136,256]{1,0:T(8,128)(2,1)S(1)}, u32[]{:S(2)}, u32[]{:S(2)}) collective-permute-start(bf16[136,256]{1,0:T(8,128)(2,1)S(1)} %prep.1), channel_id=1, source_target_pairs={{0,2},{1,3},{2,0},{3,1},{4,6},{5,7},{6,4},{7,5},{8,10},{9,11},{10,... | collective-permute-start | bytes 208904 | tf_op jit(solution)/shard_map/ppermute | solution.py:370
  8.6 0.0 collective-permute-done
  8.6 0.6 %collective-permute-start.5 = (bf16[136,256]{1,0:T(8,128)(2,1)S(1)}, bf16[136,256]{1,0:T(8,128)(2,1)S(1)}, u32[]{:S(2)}, u32[]{:S(2)}) collective-permute-start(bf16[136,256]{1,0:T(8,128)(2,1)S(1)} %collective-permute-done), channel_id=1, source_target_pairs={{0,2},{1,3},{2,0},{3,1},{4,6},{5,7},{6,4},{7,5},{8,10},{9,11},{10,... | collective-permute-start | bytes 208904 | tf_op jit(solution)/shard_map/ppermute | solution.py:370
  9.2 1.6 %collective-permute-done.1 = bf16[136,256]{1,0:T(8,128)(2,1)S(1)} collective-permute-done((bf16[136,256]{1,0:T(8,128)(2,1)S(1)}, bf16[136,256]{1,0:T(8,128)(2,1)S(1)}, u32[]{:S(2)}, u32[]{:S(2)}) %collective-permute-start.1) | collective-permute-done | bytes 69664 | tf_op jit(solution)/shard_map/ppermute | solution.py:370
  10.8 1.5 %collective-permute-start.6 = (bf16[136,256]{1,0:T(8,128)(2,1)S(1)}, bf16[136,256]{1,0:T(8,128)(2,1)S(1)}, u32[]{:S(2)}, u32[]{:S(2)}) collective-permute-start(bf16[136,256]{1,0:T(8,128)(2,1)S(1)} %collective-permute-done.1), channel_id=1, source_target_pairs={{0,2},{1,3},{2,0},{3,1},{4,6},{5,7},{6,4},{7,5},{8,10},{9,11},{10,... | collective-permute-start | bytes 208904 | tf_op jit(solution)/shard_map/ppermute | solution.py:370
  12.3 0.6 %collective-permute-done.2 = bf16[136,256]{1,0:T(8,128)(2,1)S(1)} collective-permute-done((bf16[136,256]{1,0:T(8,128)(2,1)S(1)}, bf16[136,256]{1,0:T(8,128)(2,1)S(1)}, u32[]{:S(2)}, u32[]{:S(2)}) %collective-permute-start.2) | collective-permute-done | bytes 69664 | tf_op jit(solution)/shard_map/ppermute | solution.py:370
  12.9 0.0 collective-permute-start.3
  12.9 2.2 %pairs.1.pairs_ref = s32[265]{0:T(512)S(1)} custom-call(s32[1]{0:T(128)} %bitcast.own_ref, s32[16,16]{1,0:T(8,128)} %bins_ref.1, s32[16]{0:T(128)} %owner_ref.1), custom_call_target="tpu_custom_call" | custom-call | flops 10000000 | bytes 1048576 | tf_op jit(solution)/shard_map/pairs/pallas_call | solution.py:120
  15.1 1.7 %collective-permute-start.7 = (bf16[136,256]{1,0:T(8,128)(2,1)S(1)}, bf16[136,256]{1,0:T(8,128)(2,1)S(1)}, u32[]{:S(2)}, u32[]{:S(2)}) collective-permute-start(bf16[136,256]{1,0:T(8,128)(2,1)S(1)} %collective-permute-done.2), channel_id=1, source_target_pairs={{0,3},{1,2},{2,1},{3,0},{4,7},{5,6},{6,5},{7,4},{8,11},{9,10},{10,... | collective-permute-start | bytes 208904 | tf_op jit(solution)/shard_map/ppermute | solution.py:370
  16.8 0.0 collective-permute-done.4
  16.8 0.0 collective-permute-done.5
  16.8 0.0 collective-permute-done.6
  16.8 0.1 collective-permute-start.8
  16.9 2.1 %collective-permute-done.7 = bf16[136,256]{1,0:T(8,128)(2,1)S(1)} collective-permute-done((bf16[136,256]{1,0:T(8,128)(2,1)S(1)}, bf16[136,256]{1,0:T(8,128)(2,1)S(1)}, u32[]{:S(2)}, u32[]{:S(2)}) %collective-permute-start.7) | collective-permute-done | bytes 69664 | tf_op jit(solution)/shard_map/ppermute | solution.py:370
  19.0 0.5 %collective-permute-start.9 = (bf16[136,256]{1,0:T(8,128)(2,1)S(1)}, bf16[136,256]{1,0:T(8,128)(2,1)S(1)}, u32[]{:S(2)}, u32[]{:S(2)}) collective-permute-start(bf16[136,256]{1,0:T(8,128)(2,1)S(1)} %collective-permute-done.7), channel_id=1, source_target_pairs={{0,1},{1,0},{2,3},{3,2},{4,5},{5,4},{6,7},{7,6},{8,9},{9,8},{10,11... | collective-permute-start | bytes 208904 | tf_op jit(solution)/shard_map/ppermute | solution.py:370
  19.5 0.0 collective-permute-done.3
  19.5 0.3 turn.1.a0_ref
  19.8 0.7 %early.1 = (bf16[512,512]{1,0:T(8,128)(2,1)S(1)}, f32[16,128,256]{2,1,0:T(8,128)S(1)}) custom-call(s32[265]{0:T(512)S(1)} %pairs.1.pairs_ref, bf16[4,136,256]{2,1,0:T(8,128)(2,1)S(1)} %get-tuple-element.88.x_ref.column_ref, bf16[4,136,256]{2,1,0:T(8,128)(2,1)S(1)} %get-tuple-element.87.side_ref), custom_call_target="tpu_custom_call" | custom-call | flops 32000000 | bytes 4194304 | tf_op jit(solution)/shard_map/early/pallas_call | solution.py:237
  20.5 0.6 %plane.1 = (bf16[512,512]{1,0:T(8,128)(2,1)S(1)}, f32[16,128,256]{2,1,0:T(8,128)S(1)}) custom-call(s32[265]{0:T(512)S(1)} %pairs.1.pairs_ref, bf16[4,136,256]{2,1,0:T(8,128)(2,1)S(1)} %pad_maximum_fusion.plane_ref, f32[16,128,256]{2,1,0:T(8,128)S(1)} %get-tuple-element.82._), custom_call_target="tpu_custom_call", output_to_operand_aliasing={{1}: (2, {})} | custom-call | flops 16000000 | bytes 2097152 | tf_op jit(solution)/shard_map/plane/pallas_call | solution.py:261
  21.1 0.0 collective-permute-done.9
  21.1 0.0 collective-permute-done.8
  21.2 4.5 %stack.17 = (f32[1,16640]{1,0:T(1,128)}, f32[16,128,256]{2,1,0:T(8,128)S(1)}) custom-call(s32[265]{0:T(512)S(1)} %pairs.1.pairs_ref, bf16[512,512]{1,0:T(8,128)(2,1)S(1)} %turn.1.a0_ref, bf16[512,512]{1,0:T(8,128)(2,1)S(1)} %get-tuple-element.83.a1_ref, bf16[512,512]{1,0:T(8,128)(2,1)S(1)} %get-tuple-element.84.a2_ref, ...), custom_call_target="tpu_custom_call", output_to_operand_aliasing={{1}: (4, {})} | custom-call | tf_op jit(solution)/shard_map/stack/pallas_call | solution.py:340
  (8 shorter events, 0.2 us)
Async XLA Ops:
  1.3 7.3 %collective-permute-start = (bf16[136,256]{1,0:T(8,128)(2,1)S(1)}, bf16[136,256]{1,0:T(8,128)(2,1)S(1)}, u32[]{:S(2)}, u32[]{:S(2)}) collective-permute-start(bf16[136,256]{1,0:T(8,128)(2,1)S(1)} %prep.1), channel_id=1, source_target_pairs={{0,4},{1,5},{2,6},{3,7},{4,0},{5,1},{6,2},{7,3},{8,12},{9,13},{10,... | collective-permute-start | bytes 208904 | tf_op jit(solution)/shard_map/ppermute | solution.py:370
  4.5 6.3 %collective-permute-start.1 = (bf16[136,256]{1,0:T(8,128)(2,1)S(1)}, bf16[136,256]{1,0:T(8,128)(2,1)S(1)}, u32[]{:S(2)}, u32[]{:S(2)}) collective-permute-start(bf16[136,256]{1,0:T(8,128)(2,1)S(1)} %prep.1), channel_id=1, source_target_pairs={{0,8},{1,9},{2,10},{3,11},{4,12},{5,13},{6,14},{7,15},{8,0},{9,1},... | collective-permute-start | bytes 208904 | tf_op jit(solution)/shard_map/ppermute | solution.py:370
  7.0 5.8 %collective-permute-start.2 = (bf16[136,256]{1,0:T(8,128)(2,1)S(1)}, bf16[136,256]{1,0:T(8,128)(2,1)S(1)}, u32[]{:S(2)}, u32[]{:S(2)}) collective-permute-start(bf16[136,256]{1,0:T(8,128)(2,1)S(1)} %prep.1), channel_id=1, source_target_pairs={{0,13},{1,12},{2,15},{3,14},{4,9},{5,8},{6,11},{7,10},{8,5},{9,4},... | collective-permute-start | bytes 208904 | tf_op jit(solution)/shard_map/ppermute | solution.py:370
  7.1 9.7 %collective-permute-start.4 = (bf16[136,256]{1,0:T(8,128)(2,1)S(1)}, bf16[136,256]{1,0:T(8,128)(2,1)S(1)}, u32[]{:S(2)}, u32[]{:S(2)}) collective-permute-start(bf16[136,256]{1,0:T(8,128)(2,1)S(1)} %prep.1), channel_id=1, source_target_pairs={{0,2},{1,3},{2,0},{3,1},{4,6},{5,7},{6,4},{7,5},{8,10},{9,11},{10,... | collective-permute-start | bytes 208904 | tf_op jit(solution)/shard_map/ppermute | solution.py:370
  8.6 8.2 %collective-permute-start.5 = (bf16[136,256]{1,0:T(8,128)(2,1)S(1)}, bf16[136,256]{1,0:T(8,128)(2,1)S(1)}, u32[]{:S(2)}, u32[]{:S(2)}) collective-permute-start(bf16[136,256]{1,0:T(8,128)(2,1)S(1)} %collective-permute-done), channel_id=1, source_target_pairs={{0,2},{1,3},{2,0},{3,1},{4,6},{5,7},{6,4},{7,5},{8,10},{9,11},{10,... | collective-permute-start | bytes 208904 | tf_op jit(solution)/shard_map/ppermute | solution.py:370
  10.8 6.0 %collective-permute-start.6 = (bf16[136,256]{1,0:T(8,128)(2,1)S(1)}, bf16[136,256]{1,0:T(8,128)(2,1)S(1)}, u32[]{:S(2)}, u32[]{:S(2)}) collective-permute-start(bf16[136,256]{1,0:T(8,128)(2,1)S(1)} %collective-permute-done.1), channel_id=1, source_target_pairs={{0,2},{1,3},{2,0},{3,1},{4,6},{5,7},{6,4},{7,5},{8,10},{9,11},{10,... | collective-permute-start | bytes 208904 | tf_op jit(solution)/shard_map/ppermute | solution.py:370
  12.9 6.6 %collective-permute-start.3 = (bf16[4,136,256]{2,1,0:T(8,128)(2,1)S(1)}, bf16[4,136,256]{2,1,0:T(8,128)(2,1)S(1)}, u32[]{:S(2)}, u32[]{:S(2)}) collective-permute-start(bf16[4,136,256]{2,1,0:T(8,128)(2,1)S(1)} %bitcast_dynamic-update-slice_fusion.1), channel_id=1, source_target_pairs={{0,1},{1,0},{2,3},{3,2},{4,5},{5,4},{6,7},{7,6},{8,9},{9,8},{10,11... | collective-permute-start | bytes 835592 | tf_op jit(solution)/shard_map/ppermute | solution.py:370
  15.1 3.9 %collective-permute-start.7 = (bf16[136,256]{1,0:T(8,128)(2,1)S(1)}, bf16[136,256]{1,0:T(8,128)(2,1)S(1)}, u32[]{:S(2)}, u32[]{:S(2)}) collective-permute-start(bf16[136,256]{1,0:T(8,128)(2,1)S(1)} %collective-permute-done.2), channel_id=1, source_target_pairs={{0,3},{1,2},{2,1},{3,0},{4,7},{5,6},{6,5},{7,4},{8,11},{9,10},{10,... | collective-permute-start | bytes 208904 | tf_op jit(solution)/shard_map/ppermute | solution.py:370
  16.8 4.3 %collective-permute-start.8 = (bf16[3,136,256]{2,1,0:T(8,128)(2,1)S(1)}, bf16[3,136,256]{2,1,0:T(8,128)(2,1)S(1)}, u32[]{:S(2)}, u32[]{:S(2)}) collective-permute-start(bf16[3,136,256]{2,1,0:T(8,128)(2,1)S(1)} %pad_maximum_fusion.2), channel_id=1, source_target_pairs={{0,1},{1,0},{2,3},{3,2},{4,5},{5,4},{6,7},{7,6},{8,9},{9,8},{10,11... | collective-permute-start | bytes 626696 | tf_op jit(solution)/shard_map/ppermute | solution.py:370
  19.0 2.1 %collective-permute-start.9 = (bf16[136,256]{1,0:T(8,128)(2,1)S(1)}, bf16[136,256]{1,0:T(8,128)(2,1)S(1)}, u32[]{:S(2)}, u32[]{:S(2)}) collective-permute-start(bf16[136,256]{1,0:T(8,128)(2,1)S(1)} %collective-permute-done.7), channel_id=1, source_target_pairs={{0,1},{1,0},{2,3},{3,2},{4,5},{5,4},{6,7},{7,6},{8,9},{9,8},{10,11... | collective-permute-start | bytes 208904 | tf_op jit(solution)/shard_map/ppermute | solution.py:370
